TPU v7x, 512 devices: a whole 4x4x16 slice. The times are simulated.
512 devices in a mesh: gx: 8 (over y, core), gy: 4 (over z_lo), gz: 16 (over z_hi, x).
Axes of the slice: x: 4, y: 4, z: 16 (z_hi: 4, z_lo: 4; z = z_hi * 4 + z_lo), core: 2. Of those that a mesh axis runs over, the one named last changes fastest.
Arguments:
- source: bfloat16 [32, 96, 8192], P('gx', 'gy', 'gz'), may hold values from -6 to 6
- tangent: bfloat16 [32, 96, 8192], P('gx', 'gy', 'gz'), may hold values from -6 to 6
- first_weight: bfloat16 [3, 3, 3, 64, 64], replicated, may hold values from -0.15625 to 0.15625
- first_bias: float32 [64], replicated, may hold values from -3 to 3
- second_weight: bfloat16 [3, 3, 3, 64, 64], replicated, may hold values from -0.15625 to 0.15625
- second_bias: float32 [64], replicated, may hold values from -3 to 3
Outputs:
- result: bfloat16 [32, 96, 8192], P('gx', 'gy', 'gz')
- result_tangent: bfloat16 [32, 96, 8192], P('gx', 'gy', 'gz')
All inputs are finite; a program needn't handle non-finite values.
Results may differ from a plain program's by a relative error of at most 0.0052.
Values may be sent and summed in bfloat16 or wider, within the bound.
No kernel may reach another device: no remote copies, remote signals or barrier semaphores. Data moves between devices by JAX's collectives and lax.ppermute only.
A program may use at most 64 MiB of HBM per device.

v0:
```python
import jax
import jax.numpy as jnp
import numpy as np
from jax import lax
from jax.sharding import PartitionSpec as P


def padded_2(cells, sides, width):
    for axis, dim in sides:
        count = lax.axis_size(axis)
        ends = count - 1
        head = lax.slice_in_dim(cells, 0, width, axis=dim)
        tail = lax.slice_in_dim(cells, cells.shape[dim] - width, cells.shape[dim], axis=dim)
        cells = jnp.concatenate(
            [
                lax.ppermute(tail, axis, [(i, (i + 1) % count) for i in range(ends)]),
                cells,
                lax.ppermute(head, axis, [((i + 1) % count, i) for i in range(ends)]),
            ],
            axis=dim,
        )
    return cells


def pair_table():
    table = np.zeros((3, 2, 2, 3), np.float32)
    for shift in range(3):
        for inner in range(2):
            for outer in range(2):
                offset = 2 * (shift - 1) + inner - outer + 1
                if 0 <= offset <= 2:
                    table[shift, inner, outer, offset] = 1.0
    return table


def pair_kernels(weight):
    width = weight.shape[3]
    mats = jnp.einsum("kijz,abzco->abkicjo", jnp.asarray(pair_table()), weight.astype(jnp.float32))
    return mats.reshape(3, 3, 3, 2 * width, 2 * width).astype(jnp.bfloat16)


def convolve(padded, kernels, out_x, out_y, pairs):
    lanes = kernels.shape[3]
    view = padded.reshape(2, out_x + 2, out_y + 2, pairs + 2, lanes)
    total = jnp.zeros((2, out_x, out_y, pairs, lanes), jnp.float32)
    for ox in range(3):
        for oy in range(3):
            for oz in range(3):
                window = view[:, ox : ox + out_x, oy : oy + out_y, oz : oz + pairs, :]
                total = total + jnp.einsum(
                    "sabcl,lm->sabcm",
                    window,
                    kernels[ox, oy, oz],
                    preferred_element_type=jnp.float32,
                )
    return total


def silu_slope(pre):
    sig = jax.nn.sigmoid(pre)
    return sig * (1.0 + pre * (1.0 - sig))


def width_pad(field, lanes):
    return padded_2(field, (("gz", 3),), lanes)


def plane_pad(field):
    return padded_2(field, (("gx", 1), ("gy", 2)), 1)


def shards(source, tangent, first_weight, first_bias, second_weight, second_bias):
    depth, height, flat = source.shape
    width = first_weight.shape[3]
    lanes = 2 * width
    pairs = flat // lanes
    kernels_one = pair_kernels(first_weight)
    kernels_two = pair_kernels(second_weight)
    bias_one = jnp.concatenate([first_bias, first_bias])
    bias_two = jnp.concatenate([second_bias, second_bias])
    stacked = jnp.stack([source, tangent])
    out_x, out_y = (depth, height)
    first = convolve(width_pad(plane_pad(stacked), lanes), kernels_one, out_x, out_y, pairs)
    inside = jnp.ones((1, 1, 1, 1), jnp.float32)
    pre_one = first[0] + bias_one
    hidden = (jax.nn.silu(pre_one) * inside).astype(jnp.bfloat16)
    hidden_tangent = (silu_slope(pre_one) * first[1] * inside).astype(jnp.bfloat16)
    layer = jnp.stack([hidden, hidden_tangent]).reshape(2, out_x, out_y, flat)
    padded_two = width_pad(plane_pad(layer), lanes)
    second = convolve(padded_two, kernels_two, depth, height, pairs)
    pre_two = second[0] + bias_two
    result = jax.nn.silu(pre_two).astype(jnp.bfloat16).reshape(depth, height, flat)
    result_tangent = (
        (silu_slope(pre_two) * second[1]).astype(jnp.bfloat16).reshape(depth, height, flat)
    )
    return (result, result_tangent)


def solution(mesh):
    return jax.shard_map(
        shards,
        mesh=mesh,
        in_specs=(P("gx", "gy", "gz"), P("gx", "gy", "gz"), P(), P(), P(), P()),
        out_specs=(P("gx", "gy", "gz"), P("gx", "gy", "gz")),
        check_vma=False,
    )
```

profile of v0, /device:TPU:15, one launch (start us, length us, event | category | flops | bytes accessed | tf_op | source)
XLA Modules:
  0.0 109.1 jit_solution(7714829145221628141)
XLA Ops:
  1.5 3.8 %collective-permute-start = (bf16[2,1,24,512]{3,2,1,0:T(8,128)(2,1)S(1)}, bf16[2,1,24,512]{3,2,1,0:T(8,128)(2,1)S(1)}, u32[]{:S(2)}, u32[]{:S(2)}) collective-permute-start(bf16[2,1,24,512]{3,2,1,0:T(8,128)(2,1)S(1)} %get-tuple-element.72), channel_id=1, source_target_pairs={{0,64},{64,128},{128,192},{192,256},{256,320},{320,384},{384,448},... | collective-permute-start | bytes 147464 | tf_op jit(solution)/shard_map/ppermute | solution.py:16
  5.3 1.9 %collective-permute-start.1 = (bf16[2,1,24,512]{3,2,1,0:T(8,128)(2,1)S(1)}, bf16[2,1,24,512]{3,2,1,0:T(8,128)(2,1)S(1)}, u32[]{:S(2)}, u32[]{:S(2)}) collective-permute-start(bf16[2,1,24,512]{3,2,1,0:T(8,128)(2,1)S(1)} %get-tuple-element.73), channel_id=1, source_target_pairs={{64,0},{128,64},{192,128},{256,192},{320,256},{384,320},{448,384},... | collective-permute-start | bytes 147464 | tf_op jit(solution)/shard_map/ppermute | solution.py:18
  7.2 3.5 %collective-permute-done.1 = bf16[2,1,24,512]{3,2,1,0:T(8,128)(2,1)S(1)} collective-permute-done((bf16[2,1,24,512]{3,2,1,0:T(8,128)(2,1)S(1)}, bf16[2,1,24,512]{3,2,1,0:T(8,128)(2,1)S(1)}, u32[]{:S(2)}, u32[]{:S(2)}) %collective-permute-start.1) | collective-permute-done | bytes 49184 | tf_op jit(solution)/shard_map/ppermute | solution.py:18
  11.5 3.5 %collective-permute-start.2 = (bf16[2,6,1,512]{3,2,1,0:T(2,128)(2,1)S(1)}, bf16[2,6,1,512]{3,2,1,0:T(2,128)(2,1)S(1)}, u32[]{:S(2)}, u32[]{:S(2)}) collective-permute-start(bf16[2,6,1,512]{3,2,1,0:T(2,128)(2,1)S(1)} %get-tuple-element.66), channel_id=1, source_target_pairs={{0,16},{16,32},{32,48},{1,17},{17,33},{33,49},{2,18},{18,34},{34,5... | collective-permute-start | bytes 36872 | tf_op jit(solution)/shard_map/ppermute | solution.py:16
  15.1 1.3 %collective-permute-start.3 = (bf16[2,6,1,512]{3,2,1,0:T(2,128)(2,1)S(1)}, bf16[2,6,1,512]{3,2,1,0:T(2,128)(2,1)S(1)}, u32[]{:S(2)}, u32[]{:S(2)}) collective-permute-start(bf16[2,6,1,512]{3,2,1,0:T(2,128)(2,1)S(1)} %get-tuple-element.67), channel_id=1, source_target_pairs={{16,0},{32,16},{48,32},{17,1},{33,17},{49,33},{18,2},{34,18},{50,3... | collective-permute-start | bytes 36872 | tf_op jit(solution)/shard_map/ppermute | solution.py:18
  16.4 1.8 %convert_bitcast_fusion.1 = bf16[3,3,3,2,64,2,64]{6,2,4,1,0,5,3:T(4,128)(2,1)S(1)} fusion(bf16[3,2,2,3,1,1,1]{3,0,6,5,4,2,1:T(4,128)(2,1)} %constant.58, bf16[3,3,3,64,64,1,1]{4,3,2,1,0,6,5:T(8,128)(2,1)S(1)} %bitcast.401), kind=kOutput, calls=%fused_computation.1 | convolution fusion | flops 2654208 | bytes 1105992 | tf_op jit(solution)/shard_map/kijz,abzco->abkicjo/dot_general | solution.py:38
  18.2 2.1 %copy.15 = bf16[3,3,3,2,64,2,64]{6,5,4,3,2,1,0:T(2,128)(2,1)S(1)} copy(bf16[3,3,3,2,64,2,64]{6,2,4,1,0,5,3:T(4,128)(2,1)S(1)} %convert_bitcast_fusion.1) | data formatting | bytes 1769472 | tf_op jit(solution)/shard_map/convert_element_type | solution.py:39
  21.4 8.7 %collective-permute-start.4 = (bf16[2,6,26,128]{3,2,1,0:T(8,128)(2,1)S(1)}, bf16[2,6,26,128]{3,2,1,0:T(8,128)(2,1)S(1)}, u32[]{:S(2)}, u32[]{:S(2)}) collective-permute-start(bf16[2,6,26,128]{3,2,1,0:T(8,128)(2,1)S(1)} %get-tuple-element.62), channel_id=1, source_target_pairs={{0,1},{1,2},{2,3},{3,4},{4,5},{5,6},{6,7},{7,8},{8,9},{9,10},{10,1... | collective-permute-start | bytes 239624 | tf_op jit(solution)/shard_map/ppermute | solution.py:16
  30.2 1.9 %collective-permute-start.5 = (bf16[2,6,26,128]{3,2,1,0:T(8,128)(2,1)S(1)}, bf16[2,6,26,128]{3,2,1,0:T(8,128)(2,1)S(1)}, u32[]{:S(2)}, u32[]{:S(2)}) collective-permute-start(bf16[2,6,26,128]{3,2,1,0:T(8,128)(2,1)S(1)} %get-tuple-element.63), channel_id=1, source_target_pairs={{1,0},{2,1},{3,2},{4,3},{5,4},{6,5},{7,6},{8,7},{9,8},{10,9},{11,1... | collective-permute-start | bytes 239624 | tf_op jit(solution)/shard_map/ppermute | solution.py:18
  32.3 10.2 %collective-permute-done.5 = bf16[2,6,26,128]{3,2,1,0:T(8,128)(2,1)S(1)} collective-permute-done((bf16[2,6,26,128]{3,2,1,0:T(8,128)(2,1)S(1)}, bf16[2,6,26,128]{3,2,1,0:T(8,128)(2,1)S(1)}, u32[]{:S(2)}, u32[]{:S(2)}) %collective-permute-start.5) | collective-permute-done | bytes 79904 | tf_op jit(solution)/shard_map/ppermute | solution.py:18
  43.8 1.7 %fusion.63 = (bf16[2,4,24,4,128]{4,3,2,1,0:T(4,128)(2,1)S(1)}, bf16[2,4,24,4,128]{4,3,2,1,0:T(4,128)(2,1)S(1)}, bf16[2,4,24,4,128]{4,3,2,1,0:T(4,128)(2,1)S(1)},...) fusion(bf16[2,6,26,6,128]{4,3,2,1,0:T(8,128)(2,1)S(1)} %reshape.85), kind=kLoop, calls=%fused_computation.205 | loop fusion | bytes 7471104 | tf_op jit(solution)/shard_map/slice | solution.py:49
  52.5 7.5 %collective-permute-start.6 = (bf16[2,1,24,512]{3,2,1,0:T(8,128)(2,1)S(1)}, bf16[2,1,24,512]{3,2,1,0:T(8,128)(2,1)S(1)}, u32[]{:S(2)}, u32[]{:S(2)}) collective-permute-start(bf16[2,1,24,512]{3,2,1,0:T(8,128)(2,1)S(1)} %get-tuple-element.70), channel_id=1, source_target_pairs={{0,64},{64,128},{128,192},{192,256},{256,320},{320,384},{384,448},... | collective-permute-start | bytes 147464 | tf_op jit(solution)/shard_map/ppermute | solution.py:16
  60.0 2.1 %collective-permute-start.7 = (bf16[2,1,24,512]{3,2,1,0:T(8,128)(2,1)S(1)}, bf16[2,1,24,512]{3,2,1,0:T(8,128)(2,1)S(1)}, u32[]{:S(2)}, u32[]{:S(2)}) collective-permute-start(bf16[2,1,24,512]{3,2,1,0:T(8,128)(2,1)S(1)} %get-tuple-element.71), channel_id=1, source_target_pairs={{64,0},{128,64},{192,128},{256,192},{320,256},{384,320},{448,384},... | collective-permute-start | bytes 147464 | tf_op jit(solution)/shard_map/ppermute | solution.py:18
  62.2 1.1 %convert_bitcast_fusion = bf16[3,3,3,2,64,2,64]{6,2,4,1,0,5,3:T(4,128)(2,1)S(1)} fusion(bf16[3,2,2,3,1,1,1]{3,0,6,5,4,2,1:T(4,128)(2,1)S(1)} %copy-done.4, bf16[3,3,3,64,64,1,1]{4,3,2,1,0,6,5:T(8,128)(2,1)S(1)} %bitcast.410), kind=kOutput, calls=%fused_computation | convolution fusion | flops 2654208 | bytes 1105992 | tf_op jit(solution)/shard_map/kijz,abzco->abkicjo/dot_general | solution.py:38
  63.3 2.1 %collective-permute-done.7 = bf16[2,1,24,512]{3,2,1,0:T(8,128)(2,1)S(1)} collective-permute-done((bf16[2,1,24,512]{3,2,1,0:T(8,128)(2,1)S(1)}, bf16[2,1,24,512]{3,2,1,0:T(8,128)(2,1)S(1)}, u32[]{:S(2)}, u32[]{:S(2)}) %collective-permute-start.7) | collective-permute-done | bytes 49184 | tf_op jit(solution)/shard_map/ppermute | solution.py:18
  65.5 6.6 %collective-permute-start.8 = (bf16[2,6,1,512]{3,2,1,0:T(2,128)(2,1)S(1)}, bf16[2,6,1,512]{3,2,1,0:T(2,128)(2,1)S(1)}, u32[]{:S(2)}, u32[]{:S(2)}) collective-permute-start(bf16[2,6,1,512]{3,2,1,0:T(2,128)(2,1)S(1)} %get-tuple-element.64), channel_id=1, source_target_pairs={{0,16},{16,32},{32,48},{1,17},{17,33},{33,49},{2,18},{18,34},{34,5... | collective-permute-start | bytes 36872 | tf_op jit(solution)/shard_map/ppermute | solution.py:16
  72.1 1.3 %collective-permute-start.9 = (bf16[2,6,1,512]{3,2,1,0:T(2,128)(2,1)S(1)}, bf16[2,6,1,512]{3,2,1,0:T(2,128)(2,1)S(1)}, u32[]{:S(2)}, u32[]{:S(2)}) collective-permute-start(bf16[2,6,1,512]{3,2,1,0:T(2,128)(2,1)S(1)} %get-tuple-element.65), channel_id=1, source_target_pairs={{16,0},{32,16},{48,32},{17,1},{33,17},{49,33},{18,2},{34,18},{50,3... | collective-permute-start | bytes 36872 | tf_op jit(solution)/shard_map/ppermute | solution.py:18
  73.5 3.2 %collective-permute-done.9 = bf16[2,6,1,512]{3,2,1,0:T(2,128)(2,1)S(1)} collective-permute-done((bf16[2,6,1,512]{3,2,1,0:T(2,128)(2,1)S(1)}, bf16[2,6,1,512]{3,2,1,0:T(2,128)(2,1)S(1)}, u32[]{:S(2)}, u32[]{:S(2)}) %collective-permute-start.9) | collective-permute-done | bytes 12320 | tf_op jit(solution)/shard_map/ppermute | solution.py:18
  77.4 1.9 %collective-permute-start.10 = (bf16[2,6,26,128]{3,2,1,0:T(8,128)(2,1)}, bf16[2,6,26,128]{3,2,1,0:T(8,128)(2,1)S(1)}, u32[]{:S(2)}, u32[]{:S(2)}) collective-permute-start(bf16[2,6,26,128]{3,2,1,0:T(8,128)(2,1)} %get-tuple-element.60), channel_id=1, source_target_pairs={{0,1},{1,2},{2,3},{3,4},{4,5},{5,6},{6,7},{7,8},{8,9},{9,10},{10,1... | collective-permute-start | bytes 239624 | tf_op jit(solution)/shard_map/ppermute | solution.py:16
  79.4 3.4 %collective-permute-start.11 = (bf16[2,6,26,128]{3,2,1,0:T(8,128)(2,1)}, bf16[2,6,26,128]{3,2,1,0:T(8,128)(2,1)}, u32[]{:S(2)}, u32[]{:S(2)}) collective-permute-start(bf16[2,6,26,128]{3,2,1,0:T(8,128)(2,1)} %get-tuple-element.61), channel_id=1, source_target_pairs={{1,0},{2,1},{3,2},{4,3},{5,4},{6,5},{7,6},{8,7},{9,8},{10,9},{11,1... | collective-permute-start | bytes 239624 | tf_op jit(solution)/shard_map/ppermute | solution.py:18
  82.7 2.1 %copy.47 = bf16[3,3,3,2,64,2,64]{6,5,4,3,2,1,0:T(2,128)(2,1)S(1)} copy(bf16[3,3,3,2,64,2,64]{6,2,4,1,0,5,3:T(4,128)(2,1)S(1)} %convert_bitcast_fusion) | data formatting | bytes 1769472 | tf_op jit(solution)/shard_map/convert_element_type | solution.py:39
  85.7 11.5 %collective-permute-done.11 = bf16[2,6,26,128]{3,2,1,0:T(8,128)(2,1)} collective-permute-done((bf16[2,6,26,128]{3,2,1,0:T(8,128)(2,1)}, bf16[2,6,26,128]{3,2,1,0:T(8,128)(2,1)}, u32[]{:S(2)}, u32[]{:S(2)}) %collective-permute-start.11) | collective-permute-done | bytes 79904 | tf_op jit(solution)/shard_map/ppermute | solution.py:18
  97.2 1.1 pad_maximum_fusion.1
  99.4 1.7 %fusion.61 = (bf16[2,4,24,4,128]{4,3,2,1,0:T(4,128)(2,1)S(1)}, bf16[2,4,24,4,128]{4,3,2,1,0:T(4,128)(2,1)S(1)}, bf16[2,4,24,4,128]{4,3,2,1,0:T(4,128)(2,1)S(1)},...) fusion(bf16[2,6,26,6,128]{4,3,2,1,0:T(8,128)(2,1)S(1)} %reshape.86), kind=kLoop, calls=%fused_computation.203 | loop fusion | bytes 7471104 | tf_op jit(solution)/shard_map/slice | solution.py:49
  (100 shorter events, 21.4 us)
Async XLA Ops:
  0.6 15.8 %copy-start = (bf16[3,3,3,64,64]{4,3,2,1,0:T(8,128)(2,1)S(1)}, bf16[3,3,3,64,64]{4,3,2,1,0:T(8,128)(2,1)}, u32[]{:S(2)}) copy-start(bf16[3,3,3,64,64]{4,3,2,1,0:T(8,128)(2,1)} %param.10) | copy-start | bytes 663556
  1.5 5.7 %collective-permute-start = (bf16[2,1,24,512]{3,2,1,0:T(8,128)(2,1)S(1)}, bf16[2,1,24,512]{3,2,1,0:T(8,128)(2,1)S(1)}, u32[]{:S(2)}, u32[]{:S(2)}) collective-permute-start(bf16[2,1,24,512]{3,2,1,0:T(8,128)(2,1)S(1)} %get-tuple-element.72), channel_id=1, source_target_pairs={{0,64},{64,128},{128,192},{192,256},{256,320},{320,384},{384,448},... | collective-permute-start | bytes 147464 | tf_op jit(solution)/shard_map/ppermute | solution.py:16
  5.3 5.4 %collective-permute-start.1 = (bf16[2,1,24,512]{3,2,1,0:T(8,128)(2,1)S(1)}, bf16[2,1,24,512]{3,2,1,0:T(8,128)(2,1)S(1)}, u32[]{:S(2)}, u32[]{:S(2)}) collective-permute-start(bf16[2,1,24,512]{3,2,1,0:T(8,128)(2,1)S(1)} %get-tuple-element.73), channel_id=1, source_target_pairs={{64,0},{128,64},{192,128},{256,192},{320,256},{384,320},{448,384},... | collective-permute-start | bytes 147464 | tf_op jit(solution)/shard_map/ppermute | solution.py:18
  11.5 9.7 %collective-permute-start.2 = (bf16[2,6,1,512]{3,2,1,0:T(2,128)(2,1)S(1)}, bf16[2,6,1,512]{3,2,1,0:T(2,128)(2,1)S(1)}, u32[]{:S(2)}, u32[]{:S(2)}) collective-permute-start(bf16[2,6,1,512]{3,2,1,0:T(2,128)(2,1)S(1)} %get-tuple-element.66), channel_id=1, source_target_pairs={{0,16},{16,32},{32,48},{1,17},{17,33},{33,49},{2,18},{18,34},{34,5... | collective-permute-start | bytes 36872 | tf_op jit(solution)/shard_map/ppermute | solution.py:16
  15.1 6.2 %collective-permute-start.3 = (bf16[2,6,1,512]{3,2,1,0:T(2,128)(2,1)S(1)}, bf16[2,6,1,512]{3,2,1,0:T(2,128)(2,1)S(1)}, u32[]{:S(2)}, u32[]{:S(2)}) collective-permute-start(bf16[2,6,1,512]{3,2,1,0:T(2,128)(2,1)S(1)} %get-tuple-element.67), channel_id=1, source_target_pairs={{16,0},{32,16},{48,32},{17,1},{33,17},{49,33},{18,2},{34,18},{50,3... | collective-permute-start | bytes 36872 | tf_op jit(solution)/shard_map/ppermute | solution.py:18
  20.4 0.9 copy-start.1
  20.4 0.9 copy-start.2
  20.4 11.7 %copy-start.5 = (f32[64]{0:T(128)S(1)}, f32[64]{0:T(128)}, u32[]{:S(2)}) copy-start(f32[64]{0:T(128)} %param.11) | copy-start | bytes 772
  21.4 10.9 %collective-permute-start.4 = (bf16[2,6,26,128]{3,2,1,0:T(8,128)(2,1)S(1)}, bf16[2,6,26,128]{3,2,1,0:T(8,128)(2,1)S(1)}, u32[]{:S(2)}, u32[]{:S(2)}) collective-permute-start(bf16[2,6,26,128]{3,2,1,0:T(8,128)(2,1)S(1)} %get-tuple-element.62), channel_id=1, source_target_pairs={{0,1},{1,2},{2,3},{3,4},{4,5},{5,6},{6,7},{7,8},{8,9},{9,10},{10,1... | collective-permute-start | bytes 239624 | tf_op jit(solution)/shard_map/ppermute | solution.py:16
  30.2 12.4 %collective-permute-start.5 = (bf16[2,6,26,128]{3,2,1,0:T(8,128)(2,1)S(1)}, bf16[2,6,26,128]{3,2,1,0:T(8,128)(2,1)S(1)}, u32[]{:S(2)}, u32[]{:S(2)}) collective-permute-start(bf16[2,6,26,128]{3,2,1,0:T(8,128)(2,1)S(1)} %get-tuple-element.63), channel_id=1, source_target_pairs={{1,0},{2,1},{3,2},{4,3},{5,4},{6,5},{7,6},{8,7},{9,8},{10,9},{11,1... | collective-permute-start | bytes 239624 | tf_op jit(solution)/shard_map/ppermute | solution.py:18
  52.1 10.0 %copy-start.3 = (bf16[3,3,3,64,64]{4,3,2,1,0:T(8,128)(2,1)S(1)}, bf16[3,3,3,64,64]{4,3,2,1,0:T(8,128)(2,1)}, u32[]{:S(2)}) copy-start(bf16[3,3,3,64,64]{4,3,2,1,0:T(8,128)(2,1)} %param.12) | copy-start | bytes 663556
  52.1 10.0 %copy-start.4 = (bf16[3,2,2,3,1,1,1]{3,0,6,5,4,2,1:T(4,128)(2,1)S(1)}, bf16[3,2,2,3,1,1,1]{3,0,6,5,4,2,1:T(4,128)(2,1)}, u32[]{:S(2)}) copy-start(bf16[3,2,2,3,1,1,1]{3,0,6,5,4,2,1:T(4,128)(2,1)} %constant.58) | copy-start | bytes 220
  52.5 10.8 %collective-permute-start.6 = (bf16[2,1,24,512]{3,2,1,0:T(8,128)(2,1)S(1)}, bf16[2,1,24,512]{3,2,1,0:T(8,128)(2,1)S(1)}, u32[]{:S(2)}, u32[]{:S(2)}) collective-permute-start(bf16[2,1,24,512]{3,2,1,0:T(8,128)(2,1)S(1)} %get-tuple-element.70), channel_id=1, source_target_pairs={{0,64},{64,128},{128,192},{192,256},{256,320},{320,384},{384,448},... | collective-permute-start | bytes 147464 | tf_op jit(solution)/shard_map/ppermute | solution.py:16
  60.0 5.4 %collective-permute-start.7 = (bf16[2,1,24,512]{3,2,1,0:T(8,128)(2,1)S(1)}, bf16[2,1,24,512]{3,2,1,0:T(8,128)(2,1)S(1)}, u32[]{:S(2)}, u32[]{:S(2)}) collective-permute-start(bf16[2,1,24,512]{3,2,1,0:T(8,128)(2,1)S(1)} %get-tuple-element.71), channel_id=1, source_target_pairs={{64,0},{128,64},{192,128},{256,192},{320,256},{384,320},{448,384},... | collective-permute-start | bytes 147464 | tf_op jit(solution)/shard_map/ppermute | solution.py:18
  62.1 11.3 %copy-start.6 = (f32[64]{0:T(128)S(1)}, f32[64]{0:T(128)}, u32[]{:S(2)}) copy-start(f32[64]{0:T(128)} %param.13) | copy-start | bytes 772
  65.5 8.0 %collective-permute-start.8 = (bf16[2,6,1,512]{3,2,1,0:T(2,128)(2,1)S(1)}, bf16[2,6,1,512]{3,2,1,0:T(2,128)(2,1)S(1)}, u32[]{:S(2)}, u32[]{:S(2)}) collective-permute-start(bf16[2,6,1,512]{3,2,1,0:T(2,128)(2,1)S(1)} %get-tuple-element.64), channel_id=1, source_target_pairs={{0,16},{16,32},{32,48},{1,17},{17,33},{33,49},{2,18},{18,34},{34,5... | collective-permute-start | bytes 36872 | tf_op jit(solution)/shard_map/ppermute | solution.py:16
  72.1 4.6 %collective-permute-start.9 = (bf16[2,6,1,512]{3,2,1,0:T(2,128)(2,1)S(1)}, bf16[2,6,1,512]{3,2,1,0:T(2,128)(2,1)S(1)}, u32[]{:S(2)}, u32[]{:S(2)}) collective-permute-start(bf16[2,6,1,512]{3,2,1,0:T(2,128)(2,1)S(1)} %get-tuple-element.65), channel_id=1, source_target_pairs={{16,0},{32,16},{48,32},{17,1},{33,17},{49,33},{18,2},{34,18},{50,3... | collective-permute-start | bytes 36872 | tf_op jit(solution)/shard_map/ppermute | solution.py:18
  77.4 8.3 %collective-permute-start.10 = (bf16[2,6,26,128]{3,2,1,0:T(8,128)(2,1)}, bf16[2,6,26,128]{3,2,1,0:T(8,128)(2,1)S(1)}, u32[]{:S(2)}, u32[]{:S(2)}) collective-permute-start(bf16[2,6,26,128]{3,2,1,0:T(8,128)(2,1)} %get-tuple-element.60), channel_id=1, source_target_pairs={{0,1},{1,2},{2,3},{3,4},{4,5},{5,6},{6,7},{7,8},{8,9},{9,10},{10,1... | collective-permute-start | bytes 239624 | tf_op jit(solution)/shard_map/ppermute | solution.py:16
  79.4 17.9 %collective-permute-start.11 = (bf16[2,6,26,128]{3,2,1,0:T(8,128)(2,1)}, bf16[2,6,26,128]{3,2,1,0:T(8,128)(2,1)}, u32[]{:S(2)}, u32[]{:S(2)}) collective-permute-start(bf16[2,6,26,128]{3,2,1,0:T(8,128)(2,1)} %get-tuple-element.61), channel_id=1, source_target_pairs={{1,0},{2,1},{3,2},{4,3},{5,4},{6,5},{7,6},{8,7},{9,8},{10,9},{11,1... | collective-permute-start | bytes 239624 | tf_op jit(solution)/shard_map/ppermute | solution.py:18
where the time goes:
time: 110 us; the launch traced here: 109 us
  starting transfers between devices  43.9 us (40%)
  waiting for transfers between devices  30.6 us (28%)
  matrix products  16.3 us (15%)
  local copies, waits for them, and re-layouts  11.9 us (11%)
  other arithmetic  4.88 us (4%)
  between operations  1.39 us (1%)
    ppermute x6, starting transfers between devices, padded_2(): lax.ppermute(tail, axis, [(i, (i + 1) % count) for i in range(ends)])  32 us
    ppermute x6, waiting for transfers between devices, padded_2(): lax.ppermute(head, axis, [((i + 1) % count, i) for i in range(ends)])  30.5 us
    dot_general x54, matrix products, convolve(): jnp.einsum('sabcl,lm->sabcm', window, kernels[ox, oy, oz], preferred_elem...  13.3 us
    ppermute x6, starting transfers between devices, padded_2(): lax.ppermute(head, axis, [((i + 1) % count, i) for i in range(ends)])  11.9 us
    convert_element_type x4, local copies, waits for them, and re-layouts, pair_kernels(): return mats.reshape(3, 3, 3, 2 * width, 2 * width).astype(jnp.bfloat16)  5.91 us
    slice x4, local copies, waits for them, and re-layouts, convolve(): window = view[:, ox:ox + out_x, oy:oy + out_y, oz:oz + pairs, :]  4.47 us
    dot_general x2, matrix products, pair_kernels(): jnp.einsum('kijz,abzco->abkicjo', jnp.asarray(pair_table()), weight.astyp...  2.98 us
    slice x5, other arithmetic, padded_2(): lax.slice_in_dim(cells, cells.shape[dim] - width, cells.shape[dim], axis=...  2.61 us
  transfers between devices with their start and end apart: 12, of which 6 were waited for; matrix products, arithmetic and copies ran while one was open for 8% of the time, Pallas kernels for 0%

commit v1 on v0

v1 whole, which is shorter than its diff:
```python
import functools

import jax
import jax.numpy as jnp
from jax import lax
from jax.experimental import pallas as pl
from jax.experimental.pallas import tpu as pltpu
from jax.sharding import PartitionSpec as P

F32 = jnp.float32
BF16 = jnp.bfloat16


def swap(axis, head, tail):
    count = lax.axis_size(axis)
    even = lax.axis_index(axis) % 2 == 0
    far = [(i, i + 1) for i in range(1, count - 1, 2)]
    near = [(i, i + 1) for i in range(0, count - 1, 2)]
    both = lambda pairs: pairs + [(j, i) for i, j in pairs]
    got_far = lax.ppermute(jnp.where(even, head, tail), axis, both(far))
    got_near = lax.ppermute(jnp.where(even, tail, head), axis, both(near))
    return got_far, got_near


def sides(axis, far, near):
    even = lax.axis_index(axis) % 2 == 0
    return jnp.where(even, far, near), jnp.where(even, near, far)


def weight_kernel(first, second, bias_a, bias_b, out_a, out_b, bias_out):
    for source, target in ((first, out_a), (second, out_b)):
        target[...] = jnp.zeros(target.shape, BF16)
        for dy in range(3):
            for dx in range(3):
                w = source[dx, dy]
                for k in range(2):
                    base = (dy * 4 + dx + k) * 256
                    target[base : base + 192, 128 * k : 128 * k + 64] = w
                    target[base + 64 : base + 256, 128 * k + 64 : 128 * k + 128] = w
    for row, bias in enumerate((bias_a, bias_b)):
        b = bias[...]
        bias_out[row : row + 1, :] = jnp.concatenate([b, b, b, b], axis=1)


def silu_pair(pre, direction):
    sig = jax.nn.sigmoid(pre)
    return pre * sig, sig * (1.0 + pre * (1.0 - sig)) * direction


def layer(shifted, weights, bias, planes, pairs, rows):
    parts = []
    for f in range(2):
        for xp in range(planes // 2):
            for p in range(pairs):
                parts.append(
                    jnp.concatenate(
                        [
                            shifted[dy, f, 2 * xp + j, :, 128 * p : 128 * p + 256]
                            for dy in range(3)
                            for j in range(4)
                        ],
                        axis=1,
                    )
                )
    acc = jnp.dot(jnp.concatenate(parts, axis=0), weights[...], preferred_element_type=F32)
    half = acc.shape[0] // 2
    return silu_pair(acc[:half] + bias, acc[half:])


def conv_kernel(
    place, src, tan, zf, zn, xf, xn, yf, yn, wa, wb, bias, out, out_t, ext, sh1, hid, sh2
):
    nx, ny, nz = src.shape
    pairs = nz // 128

    def pick(axis, far, near):
        even = place[3 + axis] == 1
        a, b = far[...], near[...]
        return jnp.where(even, a, b).astype(F32), jnp.where(even, b, a).astype(F32)

    zl, zr = pick(2, zf, zn)
    xl, xr = pick(0, xf, xn)
    yl, yr = pick(1, yf, yn)
    own_y = slice(2, 2 + ny)
    for f, field in enumerate((src, tan)):
        ext[f, 2 : 2 + nx, own_y, 128 : 128 + nz] = field[...].astype(F32)
    ext[:, 2 : 2 + nx, own_y, 0:128] = zl
    ext[:, 2 : 2 + nx, own_y, 128 + nz :] = zr
    ext[:, 0:2, own_y, :] = xl
    ext[:, 2 + nx :, own_y, :] = xr
    ext[:, :, 0:2, :] = yl
    ext[:, :, 2 + ny : 4 + ny, :] = yr
    rows = sh1.shape[3]
    for dy in range(3):
        sh1[dy] = ext[:, :, dy : dy + rows, :].astype(BF16)

    h, ht = layer(sh1, wa, bias[0:1, :], nx + 2, pairs + 1, rows)
    for f, value in enumerate((h, ht)):
        at = 0
        for xp in range((nx + 2) // 2):
            for p in range(pairs + 1):
                for k in range(2):
                    hid[f, 2 * xp + k, 0:rows, 128 * p : 128 * p + 128] = value[
                        at : at + rows, 128 * k : 128 * k + 128
                    ]
                at += rows

    @pl.when(place[0] == 0)
    def _():
        hid[:, 0, :, :] = jnp.zeros_like(hid[:, 0, :, :])

    @pl.when(place[0] == place[6] - 1)
    def _():
        hid[:, nx + 1, :, :] = jnp.zeros_like(hid[:, nx + 1, :, :])

    @pl.when(place[1] == 0)
    def _():
        hid[:, :, 0:1, :] = jnp.zeros_like(hid[:, :, 0:1, :])

    @pl.when(place[1] == place[7] - 1)
    def _():
        hid[:, :, ny + 1 : ny + 2, :] = jnp.zeros_like(hid[:, :, ny + 1 : ny + 2, :])

    @pl.when(place[2] == 0)
    def _():
        hid[:, :, :, 0:64] = jnp.zeros_like(hid[:, :, :, 0:64])

    @pl.when(place[2] == place[8] - 1)
    def _():
        hid[:, :, :, nz + 64 :] = jnp.zeros_like(hid[:, :, :, nz + 64 :])

    for dy in range(3):
        sh2[dy] = hid[:, :, dy : dy + rows, :].astype(BF16)
    r, rt = layer(sh2, wb, bias[1:2, :], nx, pairs, rows)
    for target, value in ((out, r), (out_t, rt)):
        at = 0
        for xp in range(nx // 2):
            for p in range(pairs):
                for k in range(2):
                    target[2 * xp + k, :, 128 * p : 128 * p + 128] = value[
                        at : at + ny, 128 * k : 128 * k + 128
                    ].astype(BF16)
                at += rows


VM = pl.BlockSpec(memory_space=pltpu.VMEM)
SM = pl.BlockSpec(memory_space=pltpu.SMEM)


def shards(source, tangent, first_weight, first_bias, second_weight, second_bias):
    nx, ny, nz = source.shape
    own = jnp.stack([source, tangent])
    names = ("gx", "gy", "gz")
    index = [lax.axis_index(a) for a in names]
    place = jnp.stack(
        [i.astype(jnp.int32) for i in index]
        + [(i % 2 == 0).astype(jnp.int32) for i in index]
        + [jnp.int32(lax.axis_size(a)) for a in names]
    )
    wa, wb, bias = pl.pallas_call(
        weight_kernel,
        in_specs=[VM] * 4,
        out_specs=[VM] * 3,
        out_shape=[
            jax.ShapeDtypeStruct((3072, 256), BF16),
            jax.ShapeDtypeStruct((3072, 256), BF16),
            jax.ShapeDtypeStruct((2, 256), F32),
        ],
        compiler_params=pltpu.CompilerParams(vmem_limit_bytes=16 << 20),
        name="weights",
    )(
        first_weight.reshape(3, 3, 192, 64),
        second_weight.reshape(3, 3, 192, 64),
        first_bias.reshape(1, 64),
        second_bias.reshape(1, 64),
    )
    zf, zn = swap("gz", own[..., :128], own[..., nz - 128 :])
    zl, zr = sides("gz", zf, zn)
    ext = jnp.concatenate([zl, own, zr], axis=3)
    xf, xn = swap("gx", ext[:, :2], ext[:, nx - 2 :])
    xl, xr = sides("gx", xf, xn)
    ends = lambda at: jnp.concatenate(
        [part[:, :, at : at + 2] for part in (xl, ext, xr)], axis=1
    )
    yf, yn = swap("gy", ends(0), ends(ny - 2))
    rows = ny + 8
    shape = jax.ShapeDtypeStruct((nx, ny, nz), BF16)
    return tuple(
        pl.pallas_call(
            conv_kernel,
            in_specs=[SM] + [VM] * 11,
            out_specs=[VM] * 2,
            out_shape=[shape, shape],
            scratch_shapes=[
                pltpu.VMEM((2, nx + 4, rows + 8, nz + 256), F32),
                pltpu.VMEM((3, 2, nx + 4, rows, nz + 256), BF16),
                pltpu.VMEM((2, nx + 2, rows + 8, nz + 128), F32),
                pltpu.VMEM((3, 2, nx + 2, rows, nz + 128), BF16),
            ],
            compiler_params=pltpu.CompilerParams(vmem_limit_bytes=40 << 20),
            name="conv",
        )(place, source, tangent, zf, zn, xf, xn, yf, yn, wa, wb, bias)
    )


def solution(mesh):
    return jax.shard_map(
        shards,
        mesh=mesh,
        in_specs=(P("gx", "gy", "gz"), P("gx", "gy", "gz"), P(), P(), P(), P()),
        out_specs=(P("gx", "gy", "gz"), P("gx", "gy", "gz")),
        check_vma=False,
    )
```

time: 110 us -> 46.3 us (0.42)
  waiting for transfers between devices: 30.6 us -> 6.23 us
  starting transfers between devices: 43.9 us -> 24.9 us
  matrix products: 16.3 us -> 0 us
  local copies, waits for them, and re-layouts: 11.9 us -> 3.88 us
  Pallas kernels: 0 us -> 6.68 us
  other arithmetic: 4.88 us -> 3.29 us
    ppermute x12 -> x6, waiting for transfers between devices: 30.6 us -> 6.23 us  [the longest x3 3.5 us: swap(): got_far = lax.ppermute(jnp.where(even, head, tail), axis, both(far))]
    ppermute x12 -> x6, starting transfers between devices: 43.9 us -> 24.9 us  [the longest x3 13.1 us: swap(): got_far = lax.ppermute(jnp.where(even, head, tail), axis, both(far))]
    dot_general x56 -> x0, matrix products: 16.3 us -> none  [the longest x54 13.3 us: convolve(): jnp.einsum('sabcl,lm->sabcm', window, kernels[ox, oy, oz], preferred_elem...]
    pallas_call x0 -> x2, Pallas kernels: none -> 6.68 us  [the longest x1 5.95 us: shards(): pl.pallas_call(conv_kernel, in_specs=[SM] + [VM] * 11, out_specs=[VM] * 2...]
    convert_element_type x4 -> x0, local copies, waits for them, and re-layouts: 5.91 us -> none  [pair_kernels(): return mats.reshape(3, 3, 3, 2 * width, 2 * width).astype(jnp.bfloat16)]
    slice x8 -> x1, local copies, waits for them, and re-layouts: 4.61 us -> 0.04 us  [shards(): part[:, :, at:at + 2]]
    unnamed x15 -> x20, local copies, waits for them, and re-layouts: 0.12 us -> 3.75 us
    slice x5 -> x0, other arithmetic: 2.61 us -> none  [padded_2(): lax.slice_in_dim(cells, cells.shape[dim] - width, cells.shape[dim], axis=...]
  transfers between devices with their start and end apart: 12 -> 6, of which waited for: 6 -> 3; matrix products, arithmetic and copies ran while one was open for 8% -> 0% of each run, Pallas kernels for 0% -> 2%
where the time goes in v1:
time: 46.3 us; the launch traced here: 45.8 us
  starting transfers between devices  24.9 us (54%)
  Pallas kernels  6.68 us (14%)
  waiting for transfers between devices  6.23 us (13%)
  local copies, waits for them, and re-layouts  3.88 us (8%)
  other arithmetic  3.29 us (7%)
  between operations  0.87 us (2%)
    ppermute x3, starting transfers between devices, swap(): got_far = lax.ppermute(jnp.where(even, head, tail), axis, both(far))  13.1 us
    ppermute x3, starting transfers between devices, swap(): got_near = lax.ppermute(jnp.where(even, tail, head), axis, both(near))  11.8 us
    pallas_call x1, Pallas kernels, shards(): pl.pallas_call(conv_kernel, in_specs=[SM] + [VM] * 11, out_specs=[VM] * 2...  5.95 us
    unnamed x20, local copies, waits for them, and re-layouts  3.75 us
    ppermute x3, waiting for transfers between devices, swap(): got_far = lax.ppermute(jnp.where(even, head, tail), axis, both(far))  3.5 us
    ppermute x3, waiting for transfers between devices, swap(): got_near = lax.ppermute(jnp.where(even, tail, head), axis, both(near))  2.73 us
    select_n x3, other arithmetic, swap(): got_near = lax.ppermute(jnp.where(even, tail, head), axis, both(near))  1.63 us
    concatenate x1, other arithmetic, shards(): ext = jnp.concatenate([zl, own, zr], axis=3)  0.98 us
  transfers between devices with their start and end apart: 6, of which 3 were waited for; matrix products, arithmetic and copies ran while one was open for 0% of the time, Pallas kernels for 2%

profile of v1, /device:TPU:15, one launch (start us, length us, event | category | flops | bytes accessed | tf_op | source)
XLA Modules:
  0.0 45.8 jit_solution(8484629903930372666)
XLA Ops:
  0.6 0.0 copy-start.1
  0.6 0.0 copy-start
  0.7 0.9 %broadcast_select_fusion.8 = (bf16[2,4,24,128]{3,2,1,0:T(8,128)(2,1)S(1)}, bf16[2,4,24,128]{3,2,1,0:T(8,128)(2,1)S(1)}, bf16[2,4,24,128]{3,2,1,0:T(8,128)(2,1)S(1)}) fusion(pred[]{:T(512)S(6)} %eq.25, bf16[1,4,24,512]{3,2,1,0:T(8,128)(2,1)} %bitcast.18, bf16[1,4,24,512]{3,2,1,0:T(8,128)(2,1)} %bitcast.15), kind=kLoop, calls=%fused_computation.21 | loop fusion | flops 221184 | bytes 344065 | tf_op jit(solution)/shard_map/jit(_where)/select_n | solution.py:21
  1.6 8.7 %collective-permute-start = (bf16[2,4,24,128]{3,2,1,0:T(8,128)(2,1)S(1)}, bf16[2,4,24,128]{3,2,1,0:T(8,128)(2,1)S(1)}, u32[]{:S(2)}, u32[]{:S(2)}) collective-permute-start(bf16[2,4,24,128]{3,2,1,0:T(8,128)(2,1)S(1)} %broadcast_select_fusion.9), channel_id=1, source_target_pairs={{1,2},{3,4},{5,6},{7,8},{9,10},{11,12},{13,14},{2,1},{4,3},{6,5},{... | collective-permute-start | bytes 147464 | tf_op jit(solution)/shard_map/ppermute | solution.py:20
  10.3 1.9 %collective-permute-start.1 = (bf16[2,4,24,128]{3,2,1,0:T(8,128)(2,1)S(1)}, bf16[2,4,24,128]{3,2,1,0:T(8,128)(2,1)S(1)}, u32[]{:S(2)}, u32[]{:S(2)}) collective-permute-start(bf16[2,4,24,128]{3,2,1,0:T(8,128)(2,1)S(1)} %get-tuple-element.11), channel_id=1, source_target_pairs={{0,1},{2,3},{4,5},{6,7},{8,9},{10,11},{12,13},{14,15},{1,0},{3,2},... | collective-permute-start | bytes 147464 | tf_op jit(solution)/shard_map/ppermute | solution.py:21
  12.3 0.2 collective-permute-done.zf
  12.4 2.7 %collective-permute-done.1.zn = bf16[2,4,24,128]{3,2,1,0:T(8,128)(2,1)S(1)} collective-permute-done((bf16[2,4,24,128]{3,2,1,0:T(8,128)(2,1)S(1)}, bf16[2,4,24,128]{3,2,1,0:T(8,128)(2,1)S(1)}, u32[]{:S(2)}, u32[]{:S(2)}) %collective-permute-start.1) | collective-permute-done | bytes 49184 | tf_op jit(solution)/shard_map/ppermute | solution.py:21
  15.2 1.0 %pad_maximum_fusion = bf16[2,4,24,768]{3,2,1,0:T(8,128)(2,1)S(1)} fusion(bf16[2,4,24,128]{3,2,1,0:T(8,128)(2,1)S(1)} %get-tuple-element.23, bf16[1,4,24,512]{3,2,1,0:T(8,128)(2,1)} %bitcast.19, bf16[1,4,24,512]{3,2,1,0:T(8,128)(2,1)} %bitcast.16, bf16[2,4,24,128]{3,2,1,0:T(8,128)(2,1)S(1)} %get-tuple-element.22), kind=kLoop, calls=%fused_computation | loop fusion | flops 1179648 | bytes 589824 | tf_op jit(solution)/shard_map/concatenate | solution.py:179
  16.2 4.0 %collective-permute-start.3 = (bf16[2,2,24,768]{3,2,1,0:T(8,128)(2,1)S(1)}, bf16[2,2,24,768]{3,2,1,0:T(8,128)(2,1)S(1)}, u32[]{:S(2)}, u32[]{:S(2)}) collective-permute-start(bf16[2,2,24,768]{3,2,1,0:T(8,128)(2,1)S(1)} %get-tuple-element.16), channel_id=1, source_target_pairs={{0,64},{128,192},{256,320},{384,448},{64,0},{192,128},{320,256},{4... | collective-permute-start | bytes 442376 | tf_op jit(solution)/shard_map/ppermute | solution.py:21
  20.2 3.1 %collective-permute-start.2 = (bf16[2,2,24,768]{3,2,1,0:T(8,128)(2,1)S(1)}, bf16[2,2,24,768]{3,2,1,0:T(8,128)(2,1)S(1)}, u32[]{:S(2)}, u32[]{:S(2)}) collective-permute-start(bf16[2,2,24,768]{3,2,1,0:T(8,128)(2,1)S(1)} %get-tuple-element.17), channel_id=1, source_target_pairs={{64,128},{192,256},{320,384},{128,64},{256,192},{384,320},{65,129}... | collective-permute-start | bytes 442376 | tf_op jit(solution)/shard_map/ppermute | solution.py:20
  23.4 0.0 collective-permute-done.3.xn
  23.4 3.3 %collective-permute-done.2.xf = bf16[2,2,24,768]{3,2,1,0:T(8,128)(2,1)S(1)} collective-permute-done((bf16[2,2,24,768]{3,2,1,0:T(8,128)(2,1)S(1)}, bf16[2,2,24,768]{3,2,1,0:T(8,128)(2,1)S(1)}, u32[]{:S(2)}, u32[]{:S(2)}) %collective-permute-start.2) | collective-permute-done | bytes 147488 | tf_op jit(solution)/shard_map/ppermute | solution.py:20
  26.8 0.7 %broadcast_select_fusion.4 = (bf16[2,8,2,768]{3,2,1,0:T(2,128)(2,1)}, bf16[2,8,2,768]{3,2,1,0:T(2,128)(2,1)S(1)}, bf16[2,8,2,768]{3,2,1,0:T(2,128)(2,1)S(1)}) fusion(pred[]{:T(512)S(6)} %eq.24, bf16[2,2,2,768]{3,2,1,0:T(2,128)(2,1)S(1)} %get-tuple-element.24, bf16[2,4,24,128]{3,2,1,0:T(8,128)(2,1)S(1)} %get-tuple-element.23, ...), kind=kLoop, calls=%fused_computation.5 | loop fusion | flops 614400 | bytes 491521 | tf_op jit(solution)/shard_map/jit(_where)/select_n | solution.py:21
  27.5 0.6 %broadcast_select_fusion.5 = bf16[2,2,8,768]{3,2,1,0:T(8,128)(2,1)} fusion(bf16[2,2,8,768]{3,2,1,0:T(8,128)(2,1)S(1)} %bitcast.26, bf16[2,2,8,768]{3,2,1,0:T(8,128)(2,1)S(1)} %bitcast.25, pred[]{:T(512)S(6)} %eq.24), kind=kLoop, calls=%fused_computation.6 | loop fusion | flops 24576 | bytes 147457 | tf_op jit(solution)/shard_map/jit(_where)/select_n | solution.py:20
  28.1 1.3 %collective-permute-start.4 = (bf16[2,8,2,768]{3,2,1,0:T(2,128)(2,1)}, bf16[2,8,2,768]{3,2,1,0:T(2,128)(2,1)}, u32[]{:S(2)}, u32[]{:S(2)}) collective-permute-start(bf16[2,8,2,768]{3,2,1,0:T(2,128)(2,1)} %bitcast.14), channel_id=1, source_target_pairs={{16,32},{32,16},{17,33},{33,17},{18,34},{34,18},{19,35},{35,19},{2... | collective-permute-start | bytes 147464 | tf_op jit(solution)/shard_map/ppermute | solution.py:20
  29.4 5.8 %collective-permute-start.5 = (bf16[2,8,2,768]{3,2,1,0:T(2,128)(2,1)}, bf16[2,8,2,768]{3,2,1,0:T(2,128)(2,1)}, u32[]{:S(2)}, u32[]{:S(2)}) collective-permute-start(bf16[2,8,2,768]{3,2,1,0:T(2,128)(2,1)} %get-tuple-element.8), channel_id=1, source_target_pairs={{0,16},{32,48},{16,0},{48,32},{1,17},{33,49},{17,1},{49,33},{2,18}... | collective-permute-start | bytes 147464 | tf_op jit(solution)/shard_map/ppermute | solution.py:21
  35.3 0.0 copy-start.4
  35.3 1.0 %copy-done.4 = bf16[3,3,3,64,64]{4,3,2,1,0:T(8,128)(2,1)S(1)} copy-done((bf16[3,3,3,64,64]{4,3,2,1,0:T(8,128)(2,1)S(1)}, bf16[3,3,3,64,64]{4,3,2,1,0:T(8,128)(2,1)}, u32[]{:S(2)}) %copy-start.4) | copy-done | bytes 221208
  36.3 1.0 %copy-done.5 = bf16[3,3,3,64,64]{4,3,2,1,0:T(8,128)(2,1)S(1)} copy-done((bf16[3,3,3,64,64]{4,3,2,1,0:T(8,128)(2,1)S(1)}, bf16[3,3,3,64,64]{4,3,2,1,0:T(8,128)(2,1)}, u32[]{:S(2)}) %copy-start.5) | copy-done | bytes 221208
  37.3 0.7 %weights.1 = (bf16[3072,256]{1,0:T(8,128)(2,1)S(1)}, bf16[3072,256]{1,0:T(8,128)(2,1)S(1)}, f32[2,256]{1,0:T(2,128)S(1)}) custom-call(bf16[3,3,192,64]{3,2,1,0:T(8,128)(2,1)S(1)} %bitcast.21, bf16[3,3,192,64]{3,2,1,0:T(8,128)(2,1)S(1)} %bitcast.22, f32[1,64]{1,0:T(1,128)S(1)} %bitcast.23, f32[1,64]{1,0:T(1,128)S(1)} %bitcast.24), custom_call_target="tpu_custom_call" | custom-call | tf_op jit(solution)/shard_map/weights/pallas_call | solution.py:160
  38.0 0.1 stack.48.place
  38.2 0.9 %copy-done.3 = bf16[2,2,24,768]{3,2,1,0:T(8,128)(2,1)S(1)} copy-done((bf16[2,2,24,768]{3,2,1,0:T(8,128)(2,1)S(1)}, bf16[2,2,24,768]{3,2,1,0:T(8,128)(2,1)}, u32[]{:S(2)}) %copy-start.3) | copy-done | bytes 147480
  39.1 0.8 %copy-done.7 = bf16[2,4,24,128]{3,2,1,0:T(8,128)(2,1)S(1)} copy-done((bf16[2,4,24,128]{3,2,1,0:T(8,128)(2,1)S(1)}, bf16[2,4,24,128]{3,2,1,0:T(8,128)(2,1)}, u32[]{:S(2)}) %copy-start.7) | copy-done | bytes 49176
  39.9 6.0 %conv.1 = (bf16[4,24,512]{2,1,0:T(8,128)(2,1)}, bf16[4,24,512]{2,1,0:T(8,128)(2,1)}) custom-call(s32[9]{0:T(128)S(1)} %stack.48.place, bf16[4,24,512]{2,1,0:T(8,128)(2,1)S(1)} %copy-done, bf16[4,24,512]{2,1,0:T(8,128)(2,1)S(1)} %copy-done.1, bf16[2,4,24,128]{3,2,1,0:T(8,128)(2,1)S(1)} %collective-permute-done.zf, bf16[2,4,24,128]{3,2,1,0:T(8,128)(2,1)S(1)} %copy-done.7, ...), custom_call_target="tpu_custom_call" | custom-call | tf_op jit(solution)/shard_map/conv/pallas_call | solution.py:189
  (20 shorter events, 0.1 us)
Async XLA Ops:
  0.6 26.1 %copy-start.1 = (bf16[4,24,512]{2,1,0:T(8,128)(2,1)S(1)}, bf16[4,24,512]{2,1,0:T(8,128)(2,1)}, u32[]{:S(2)}) copy-start(bf16[4,24,512]{2,1,0:T(8,128)(2,1)} %tan.1) | copy-start | bytes 294916
  0.6 26.1 %copy-start = (bf16[4,24,512]{2,1,0:T(8,128)(2,1)S(1)}, bf16[4,24,512]{2,1,0:T(8,128)(2,1)}, u32[]{:S(2)}) copy-start(bf16[4,24,512]{2,1,0:T(8,128)(2,1)} %src.1) | copy-start | bytes 294916
  0.7 34.6 %copy-start.8 = (f32[64]{0:T(128)S(1)}, f32[64]{0:T(128)}, u32[]{:S(2)}) copy-start(f32[64]{0:T(128)} %param.9) | copy-start | bytes 772
  0.7 34.6 %copy-start.9 = (f32[64]{0:T(128)S(1)}, f32[64]{0:T(128)}, u32[]{:S(2)}) copy-start(f32[64]{0:T(128)} %param.11) | copy-start | bytes 772
  1.6 10.9 %collective-permute-start = (bf16[2,4,24,128]{3,2,1,0:T(8,128)(2,1)S(1)}, bf16[2,4,24,128]{3,2,1,0:T(8,128)(2,1)S(1)}, u32[]{:S(2)}, u32[]{:S(2)}) collective-permute-start(bf16[2,4,24,128]{3,2,1,0:T(8,128)(2,1)S(1)} %broadcast_select_fusion.9), channel_id=1, source_target_pairs={{1,2},{3,4},{5,6},{7,8},{9,10},{11,12},{13,14},{2,1},{4,3},{6,5},{... | collective-permute-start | bytes 147464 | tf_op jit(solution)/shard_map/ppermute | solution.py:20
  10.3 4.8 %collective-permute-start.1 = (bf16[2,4,24,128]{3,2,1,0:T(8,128)(2,1)S(1)}, bf16[2,4,24,128]{3,2,1,0:T(8,128)(2,1)S(1)}, u32[]{:S(2)}, u32[]{:S(2)}) collective-permute-start(bf16[2,4,24,128]{3,2,1,0:T(8,128)(2,1)S(1)} %get-tuple-element.11), channel_id=1, source_target_pairs={{0,1},{2,3},{4,5},{6,7},{8,9},{10,11},{12,13},{14,15},{1,0},{3,2},... | collective-permute-start | bytes 147464 | tf_op jit(solution)/shard_map/ppermute | solution.py:21
  15.2 1.0 %copy-start.6 = (bf16[2,4,24,128]{3,2,1,0:T(8,128)(2,1)}, bf16[2,4,24,128]{3,2,1,0:T(8,128)(2,1)S(1)}, u32[]{:S(2)}) copy-start(bf16[2,4,24,128]{3,2,1,0:T(8,128)(2,1)S(1)} %collective-permute-done.1.zn) | copy-start | bytes 147460
  16.2 7.1 %collective-permute-start.3 = (bf16[2,2,24,768]{3,2,1,0:T(8,128)(2,1)S(1)}, bf16[2,2,24,768]{3,2,1,0:T(8,128)(2,1)S(1)}, u32[]{:S(2)}, u32[]{:S(2)}) collective-permute-start(bf16[2,2,24,768]{3,2,1,0:T(8,128)(2,1)S(1)} %get-tuple-element.16), channel_id=1, source_target_pairs={{0,64},{128,192},{256,320},{384,448},{64,0},{192,128},{320,256},{4... | collective-permute-start | bytes 442376 | tf_op jit(solution)/shard_map/ppermute | solution.py:21
  20.2 6.5 %collective-permute-start.2 = (bf16[2,2,24,768]{3,2,1,0:T(8,128)(2,1)S(1)}, bf16[2,2,24,768]{3,2,1,0:T(8,128)(2,1)S(1)}, u32[]{:S(2)}, u32[]{:S(2)}) collective-permute-start(bf16[2,2,24,768]{3,2,1,0:T(8,128)(2,1)S(1)} %get-tuple-element.17), channel_id=1, source_target_pairs={{64,128},{192,256},{320,384},{128,64},{256,192},{384,320},{65,129}... | collective-permute-start | bytes 442376 | tf_op jit(solution)/shard_map/ppermute | solution.py:20
  26.7 8.6 %copy-start.2 = (bf16[2,2,24,768]{3,2,1,0:T(8,128)(2,1)}, bf16[2,2,24,768]{3,2,1,0:T(8,128)(2,1)S(1)}, u32[]{:S(2)}) copy-start(bf16[2,2,24,768]{3,2,1,0:T(8,128)(2,1)S(1)} %collective-permute-done.2.xf) | copy-start | bytes 442372
  28.1 10.0 %collective-permute-start.4 = (bf16[2,8,2,768]{3,2,1,0:T(2,128)(2,1)}, bf16[2,8,2,768]{3,2,1,0:T(2,128)(2,1)}, u32[]{:S(2)}, u32[]{:S(2)}) collective-permute-start(bf16[2,8,2,768]{3,2,1,0:T(2,128)(2,1)} %bitcast.14), channel_id=1, source_target_pairs={{16,32},{32,16},{17,33},{33,17},{18,34},{34,18},{19,35},{35,19},{2... | collective-permute-start | bytes 147464 | tf_op jit(solution)/shard_map/ppermute | solution.py:20
  29.4 8.7 %collective-permute-start.5 = (bf16[2,8,2,768]{3,2,1,0:T(2,128)(2,1)}, bf16[2,8,2,768]{3,2,1,0:T(2,128)(2,1)}, u32[]{:S(2)}, u32[]{:S(2)}) collective-permute-start(bf16[2,8,2,768]{3,2,1,0:T(2,128)(2,1)} %get-tuple-element.8), channel_id=1, source_target_pairs={{0,16},{32,48},{16,0},{48,32},{1,17},{33,49},{17,1},{49,33},{2,18}... | collective-permute-start | bytes 147464 | tf_op jit(solution)/shard_map/ppermute | solution.py:21
  35.3 1.0 %copy-start.4 = (bf16[3,3,3,64,64]{4,3,2,1,0:T(8,128)(2,1)S(1)}, bf16[3,3,3,64,64]{4,3,2,1,0:T(8,128)(2,1)}, u32[]{:S(2)}) copy-start(bf16[3,3,3,64,64]{4,3,2,1,0:T(8,128)(2,1)} %param.8) | copy-start | bytes 663556
  36.3 1.0 %copy-start.5 = (bf16[3,3,3,64,64]{4,3,2,1,0:T(8,128)(2,1)S(1)}, bf16[3,3,3,64,64]{4,3,2,1,0:T(8,128)(2,1)}, u32[]{:S(2)}) copy-start(bf16[3,3,3,64,64]{4,3,2,1,0:T(8,128)(2,1)} %param.10) | copy-start | bytes 663556
  38.1 0.9 %copy-start.3 = (bf16[2,2,24,768]{3,2,1,0:T(8,128)(2,1)S(1)}, bf16[2,2,24,768]{3,2,1,0:T(8,128)(2,1)}, u32[]{:S(2)}) copy-start(bf16[2,2,24,768]{3,2,1,0:T(8,128)(2,1)} %copy-done.2) | copy-start | bytes 442372
  39.1 0.8 %copy-start.7 = (bf16[2,4,24,128]{3,2,1,0:T(8,128)(2,1)S(1)}, bf16[2,4,24,128]{3,2,1,0:T(8,128)(2,1)}, u32[]{:S(2)}) copy-start(bf16[2,4,24,128]{3,2,1,0:T(8,128)(2,1)} %copy-done.6) | copy-start | bytes 147460

commit v2 on v0

v2 whole, which is shorter than its diff:
```python
import jax
import jax.numpy as jnp
from jax import lax
from jax.experimental import pallas as pl
from jax.experimental.pallas import tpu as pltpu
from jax.sharding import PartitionSpec as P


F32 = jnp.float32
BF16 = jnp.bfloat16
ROWS = 32
VM = pl.BlockSpec(memory_space=pltpu.VMEM)
SM = pl.BlockSpec(memory_space=pltpu.SMEM)
HB = pl.BlockSpec(memory_space=pl.ANY)


def swap_pairs(axis, first):
    count = lax.axis_size(axis)
    pairs = [(i, i + 1) for i in range(first, count - 1, 2)]
    return pairs + [(j, i) for i, j in pairs]


def swap(axis, head, tail):
    even = lax.axis_index(axis) % 2 == 0
    to_far = jnp.where(even, head, tail)
    to_near = jnp.where(even, tail, head)
    far = lax.ppermute(to_far, axis, swap_pairs(axis, 1))
    near = lax.ppermute(to_near, axis, swap_pairs(axis, 0))
    return far, near


def sides(axis, far, near):
    even = lax.axis_index(axis) % 2 == 0
    return jnp.where(even, far, near), jnp.where(even, near, far)


def pick(even, far, near):
    a, b = far[...], near[...]
    return jnp.where(even, a, b).astype(F32), jnp.where(even, b, a).astype(F32)


def weight_kernel(first, second, bias_a, bias_b, out_a, out_b, bias_out, raw, sems):
    copies = [
        pltpu.make_async_copy(source, raw.at[n], sems.at[n])
        for n, source in enumerate((first, second))
    ]
    for copy in copies:
        copy.start()
    for row, bias in enumerate((bias_a, bias_b)):
        b = bias[...]
        bias_out[row : row + 1, :] = jnp.concatenate([b, b, b, b], axis=1)
    for n, target in enumerate((out_a, out_b)):
        target[...] = jnp.zeros(target.shape, BF16)
        copies[n].wait()
        for dy in range(3):
            for dx in range(3):
                w = raw[n, dx, dy]
                for k in range(2):
                    base = ((dx + k) * 3 + dy) * 256
                    target[base : base + 192, 128 * k : 128 * k + 64] = w
                    target[base + 64 : base + 256, 128 * k + 64 : 128 * k + 128] = w


def taps(read, starts, pairs):
    return jnp.concatenate(
        [
            jnp.concatenate(
                [read(dy, x, p) for x in planes for dy in range(3)], axis=1
            )
            for planes in starts
            for p in range(pairs)
        ],
        axis=0,
    )


def dot(lhs, rhs):
    return jnp.dot(lhs, rhs, preferred_element_type=F32)


def shift_rows(ext, shifted):
    for dy in range(3):
        for x in range(shifted.shape[1]):
            both = ext[:, x, dy : dy + ROWS, :].astype(BF16)
            shifted[dy, x] = both.reshape(2 * ROWS, both.shape[2])


def own_kernel(place, own, zf, zn, wa, acc, ext, shifted):
    nx, ny, nz = own.shape[1:]
    zl, zr = pick(place[5] == 1, zf, zn)
    ext[:, :, 0:2, :] = jnp.zeros_like(ext[:, :, 0:2, :])
    ext[:, :, 2 + ny :, :] = jnp.zeros_like(ext[:, :, 2 + ny :, :])
    ext[:, :, 2 : 2 + ny, 128 : 128 + nz] = own[...].astype(F32)
    ext[:, :, 2 : 2 + ny, 0:128] = zl
    ext[:, :, 2 : 2 + ny, 128 + nz :] = zr
    shift_rows(ext, shifted)
    read = lambda dy, x, p: shifted[dy, x, :, 128 * p : 128 * p + 256]
    pairs = nz // 128 + 1
    half = wa.shape[0] // 2
    size = pairs * 2 * ROWS
    last = nx // 2
    low = dot(taps(read, [(2 * i, 2 * i + 1) for i in range(last)], pairs), wa[:half])
    high = dot(taps(read, [(2 * i, 2 * i + 1) for i in range(last)], pairs), wa[half:])
    acc[0] = high[:size]
    for i in range(1, last):
        acc[i] = high[i * size : i * size + size] + low[(i - 1) * size : i * size]
    acc[last] = low[(last - 1) * size :]


def side_kernel(place, xf, xn, wa, acc, out, ext, shifted):
    ny = xf.shape[2]
    xl, xr = pick(place[3] == 1, xf, xn)
    ext[:, :, 0:2, :] = jnp.zeros_like(ext[:, :, 0:2, :])
    ext[:, :, 2 + ny :, :] = jnp.zeros_like(ext[:, :, 2 + ny :, :])
    ext[:, 0:2, 2 : 2 + ny, :] = xl
    ext[:, 2:4, 2 : 2 + ny, :] = xr
    shift_rows(ext, shifted)
    read = lambda dy, x, p: shifted[dy, x, :, 128 * p : 128 * p + 256]
    pairs = ext.shape[3] // 128 - 1
    half = wa.shape[0] // 2
    out[0] = acc[0] + dot(taps(read, [(0, 1)], pairs), wa[:half])
    out[1] = acc[acc.shape[0] - 1] + dot(taps(read, [(2, 3)], pairs), wa[half:])


def silu_pair(pre, direction):
    sig = jax.nn.sigmoid(pre)
    return pre * sig, sig * (1.0 + pre * (1.0 - sig)) * direction


def last_kernel(
    place, yf, yn, mid, ends, wa, wb, bias, out, out_t, edge, acc, hid, shifted
):
    nx, ny, nz = out.shape
    pairs = nz // 128
    half = wa.shape[0] // 2
    yl, yr = pick(place[4] == 1, yf, yn)
    edge[...] = jnp.zeros_like(edge)
    edge[0, :, :, 0:2, :] = yl
    edge[1, :, :, 0:1, :] = yl[:, :, 1:2]
    edge[1, :, :, 3:4, :] = yr[:, :, 0:1]
    edge[2, :, :, 2:4, :] = yr

    def read_edge(dy, x, p):
        part = edge[dy, :, x, :, 128 * p : 128 * p + 256]
        return part.reshape(16, 256).astype(BF16)

    blocks = nx // 2 + 1
    low = taps(read_edge, [(2 * i, 2 * i + 1) for i in range(blocks)], pairs + 1)
    high = taps(read_edge, [(2 * i + 2, 2 * i + 3) for i in range(blocks)], pairs + 1)
    extra = dot(low, wa[:half]) + dot(high, wa[half:])
    for i in range(blocks):
        if i == 0:
            acc[i] = ends[0]
        elif i == blocks - 1:
            acc[i] = ends[1]
        else:
            acc[i] = mid[i]
        for g in range(2 * (pairs + 1)):
            at = (i * 2 * (pairs + 1) + g) * 8
            top = ROWS * g
            low_end = top + ny
            acc[i, top : top + 2, :] += extra[at : at + 2]
            acc[i, low_end : low_end + 2, :] += extra[at + 2 : at + 4]
    b = bias[0:1, :]
    for i in range(blocks):
        for p in range(pairs + 1):
            at = p * 2 * ROWS
            value = silu_pair(
                acc[i, at : at + ROWS, :] + b, acc[i, at + ROWS : at + 2 * ROWS, :]
            )
            for f in range(2):
                for k in range(2):
                    hid[f, 2 * i + k, 0:ROWS, 128 * p : 128 * p + 128] = value[f][
                        :, 128 * k : 128 * k + 128
                    ]

    def clear(when, index):
        @pl.when(when)
        def _():
            hid[index] = jnp.zeros_like(hid[index])

    every = slice(None)
    clear(place[0] == 0, (every, 0))
    clear(place[0] == place[6] - 1, (every, nx + 1))
    clear(place[1] == 0, (every, every, slice(0, 1)))
    clear(place[1] == place[7] - 1, (every, every, slice(ny + 1, ny + 2)))
    clear(place[2] == 0, (every, every, every, slice(0, 64)))
    clear(place[2] == place[8] - 1, (every, every, every, slice(nz + 64, nz + 128)))

    for dy in range(3):
        for x in range(nx + 2):
            both = jnp.concatenate([hid[f, x, dy : dy + ny, :] for f in range(2)], axis=0)
            shifted[dy, x] = both.astype(BF16)
    read = lambda dy, x, p: shifted[dy, x, :, 128 * p : 128 * p + 256]
    blocks = nx // 2
    low = taps(read, [(2 * i, 2 * i + 1) for i in range(blocks)], pairs)
    high = taps(read, [(2 * i + 2, 2 * i + 3) for i in range(blocks)], pairs)
    total = dot(low, wb[:half]) + dot(high, wb[half:])
    b = bias[1:2, :]
    for i in range(blocks):
        for p in range(pairs):
            at = (i * pairs + p) * 2 * ny
            value = silu_pair(total[at : at + ny] + b, total[at + ny : at + 2 * ny])
            for target, part in zip((out, out_t), value):
                for k in range(2):
                    target[2 * i + k, :, 128 * p : 128 * p + 128] = part[
                        :, 128 * k : 128 * k + 128
                    ].astype(BF16)


def call(kernel, ins, outs, scratch, args, mib=24):
    return pl.pallas_call(
        kernel,
        in_specs=ins,
        out_specs=[VM] * len(outs),
        out_shape=[jax.ShapeDtypeStruct(*o) for o in outs],
        scratch_shapes=scratch,
        compiler_params=pltpu.CompilerParams(vmem_limit_bytes=mib << 20),
    )(*args)


def shards(source, tangent, first_weight, first_bias, second_weight, second_bias):
    nx, ny, nz = source.shape
    own = lax.optimization_barrier(jnp.stack([source, tangent]))
    names = ("gx", "gy", "gz")
    index = [lax.axis_index(a) for a in names]
    place = jnp.stack(
        [i.astype(jnp.int32) for i in index]
        + [(i % 2 == 0).astype(jnp.int32) for i in index]
        + [jnp.int32(lax.axis_size(a)) for a in names]
    )
    wa, wb, bias = call(
        weight_kernel,
        [HB, HB, VM, VM],
        [((3072, 256), BF16), ((3072, 256), BF16), ((2, 256), F32)],
        [pltpu.VMEM((2, 3, 3, 192, 64), BF16), pltpu.SemaphoreType.DMA((2,))],
        (
            first_weight.reshape(3, 3, 192, 64),
            second_weight.reshape(3, 3, 192, 64),
            first_bias.reshape(1, 64),
            second_bias.reshape(1, 64),
        ),
    )
    zf, zn = swap("gz", own[..., :128], own[..., nz - 128 :])
    zl, zr = sides("gz", zf, zn)
    ext = jnp.concatenate([zl, own, zr], axis=3)
    xf, xn = swap("gx", ext[:, :2], ext[:, nx - 2 :])
    xl, xr = sides("gx", xf, xn)
    ends = lambda at: jnp.concatenate(
        [part[:, :, at : at + 2] for part in (xl, ext, xr)], axis=1
    )
    yf, yn = swap("gy", ends(0), ends(ny - 2))

    wide = nz + 256
    blocks = nx // 2 + 1
    size = (nz // 128 + 1) * 2 * ROWS
    work = [
        pltpu.VMEM((2, 4, ROWS + 8, wide), F32),
        pltpu.VMEM((3, 4, 2 * ROWS, wide), BF16),
    ]
    (mid,) = call(
        own_kernel,
        [SM] + [VM] * 4,
        [((blocks, size, 256), F32)],
        [
            pltpu.VMEM((2, nx, ROWS + 8, wide), F32),
            pltpu.VMEM((3, nx, 2 * ROWS, wide), BF16),
        ],
        (place, own, zf, zn, wa),
    )
    (outer,) = call(
        side_kernel,
        [SM] + [VM] * 4,
        [((2, size, 256), F32)],
        work,
        (place, xf, xn, wa, mid),
    )
    block = ((nx, ny, nz), BF16)
    return tuple(
        call(
            last_kernel,
            [SM] + [VM] * 7,
            [block, block],
            [
                pltpu.VMEM((3, 2, nx + 4, 8, wide), F32),
                pltpu.VMEM((blocks, size, 256), F32),
                pltpu.VMEM((2, nx + 2, ROWS + 8, nz + 128), F32),
                pltpu.VMEM((3, nx + 2, 2 * ny, nz + 128), BF16),
            ],
            (place, yf, yn, mid, outer, wa, wb, bias),
        )
    )


def solution(mesh):
    return jax.shard_map(
        shards,
        mesh=mesh,
        in_specs=(P("gx", "gy", "gz"), P("gx", "gy", "gz"), P(), P(), P(), P()),
        out_specs=(P("gx", "gy", "gz"), P("gx", "gy", "gz")),
        check_vma=False,
    )
```

time: 110 us -> 44.1 us (0.40)
  the two profiles are of different devices: /device:TPU:15 before, /device:TPU:6 now
where the time goes in v2:
time: 44.1 us; the launch traced here: 43.7 us
  starting transfers between devices  24.1 us (55%)
  Pallas kernels  8.24 us (19%)
  waiting for transfers between devices  5.01 us (11%)
  local copies, waits for them, and re-layouts  3.02 us (7%)
  other arithmetic  2.42 us (5%)
  between operations  0.87 us (2%)
    ppermute x3, starting transfers between devices, swap(): near = lax.ppermute(to_near, axis, swap_pairs(axis, 0))  13.1 us
    ppermute x3, starting transfers between devices, swap(): far = lax.ppermute(to_far, axis, swap_pairs(axis, 1))  11 us
    pallas_call x4, Pallas kernels, call(): pl.pallas_call(kernel, in_specs=ins, out_specs=[VM] * len(outs), out_shap...  8.24 us
    ppermute x3, waiting for transfers between devices, swap(): near = lax.ppermute(to_near, axis, swap_pairs(axis, 0))  3.44 us
    unnamed x16, local copies, waits for them, and re-layouts  2.88 us
    ppermute x3, waiting for transfers between devices, swap(): far = lax.ppermute(to_far, axis, swap_pairs(axis, 1))  1.57 us
    another operation x1, other arithmetic, shards(): own = lax.optimization_barrier(jnp.stack([source, tangent]))  0.96 us
  transfers between devices with their start and end apart: 6, of which 3 were waited for; matrix products, arithmetic and copies ran while one was open for 0% of the time, Pallas kernels for 10%

profile of v2, /device:TPU:6, one launch (start us, length us, event | category | flops | bytes accessed | tf_op | source)
XLA Modules:
  0.0 43.7 jit_solution(12994476795473998410)
XLA Ops:
  0.6 1.0 %pad_maximum_fusion.1.own = bf16[2,4,24,512]{3,2,1,0:T(8,128)(2,1)S(1)} fusion(bf16[1,4,24,512]{3,2,1,0:T(8,128)(2,1)} %bitcast.21, bf16[1,4,24,512]{3,2,1,0:T(8,128)(2,1)} %bitcast.22), kind=kLoop, calls=%fused_computation.1 | loop fusion | flops 98304 | bytes 393216 | tf_op jit(solution)/shard_map/stack | solution.py:224
  1.6 0.0 copy-start.6
  1.6 0.0 copy-start.7
  1.7 9.0 %collective-permute-start = (bf16[2,4,24,128]{3,2,1,0:T(8,128)(2,1)S(1)}, bf16[2,4,24,128]{3,2,1,0:T(8,128)(2,1)S(1)}, u32[]{:S(2)}, u32[]{:S(2)}) collective-permute-start(bf16[2,4,24,128]{3,2,1,0:T(8,128)(2,1)S(1)} %get-tuple-element.15), channel_id=1, source_target_pairs={{1,2},{3,4},{5,6},{7,8},{9,10},{11,12},{13,14},{2,1},{4,3},{6,5},{... | collective-permute-start | bytes 147464 | tf_op jit(solution)/shard_map/ppermute | solution.py:27
  10.7 1.9 %collective-permute-start.1 = (bf16[2,4,24,128]{3,2,1,0:T(8,128)(2,1)S(1)}, bf16[2,4,24,128]{3,2,1,0:T(8,128)(2,1)S(1)}, u32[]{:S(2)}, u32[]{:S(2)}) collective-permute-start(bf16[2,4,24,128]{3,2,1,0:T(8,128)(2,1)S(1)} %get-tuple-element.16), channel_id=1, source_target_pairs={{0,1},{2,3},{4,5},{6,7},{8,9},{10,11},{12,13},{14,15},{1,0},{3,2},... | collective-permute-start | bytes 147464 | tf_op jit(solution)/shard_map/ppermute | solution.py:28
  12.6 1.6 %collective-permute-done.zf = bf16[2,4,24,128]{3,2,1,0:T(8,128)(2,1)S(1)} collective-permute-done((bf16[2,4,24,128]{3,2,1,0:T(8,128)(2,1)S(1)}, bf16[2,4,24,128]{3,2,1,0:T(8,128)(2,1)S(1)}, u32[]{:S(2)}, u32[]{:S(2)}) %collective-permute-start) | collective-permute-done | bytes 49184 | tf_op jit(solution)/shard_map/ppermute | solution.py:27
  14.2 2.5 %collective-permute-done.1.zn = bf16[2,4,24,128]{3,2,1,0:T(8,128)(2,1)S(1)} collective-permute-done((bf16[2,4,24,128]{3,2,1,0:T(8,128)(2,1)S(1)}, bf16[2,4,24,128]{3,2,1,0:T(8,128)(2,1)S(1)}, u32[]{:S(2)}, u32[]{:S(2)}) %collective-permute-start.1) | collective-permute-done | bytes 49184 | tf_op jit(solution)/shard_map/ppermute | solution.py:28
  16.7 0.7 %collective-permute-start.2 = (bf16[2,2,24,768]{3,2,1,0:T(8,128)(2,1)S(1)}, bf16[2,2,24,768]{3,2,1,0:T(8,128)(2,1)S(1)}, u32[]{:S(2)}, u32[]{:S(2)}) collective-permute-start(bf16[2,2,24,768]{3,2,1,0:T(8,128)(2,1)S(1)} %get-tuple-element.13), channel_id=1, source_target_pairs={{64,128},{192,256},{320,384},{128,64},{256,192},{384,320},{65,129}... | collective-permute-start | bytes 442376 | tf_op jit(solution)/shard_map/ppermute | solution.py:27
  17.4 4.8 %collective-permute-start.3 = (bf16[2,2,24,768]{3,2,1,0:T(8,128)(2,1)S(1)}, bf16[2,2,24,768]{3,2,1,0:T(8,128)(2,1)S(1)}, u32[]{:S(2)}, u32[]{:S(2)}) collective-permute-start(bf16[2,2,24,768]{3,2,1,0:T(8,128)(2,1)S(1)} %get-tuple-element.14), channel_id=1, source_target_pairs={{0,64},{128,192},{256,320},{384,448},{64,0},{192,128},{320,256},{4... | collective-permute-start | bytes 442376 | tf_op jit(solution)/shard_map/ppermute | solution.py:28
  22.3 1.0 %collective-permute-done.3.xn = bf16[2,2,24,768]{3,2,1,0:T(8,128)(2,1)S(1)} collective-permute-done((bf16[2,2,24,768]{3,2,1,0:T(8,128)(2,1)S(1)}, bf16[2,2,24,768]{3,2,1,0:T(8,128)(2,1)S(1)}, u32[]{:S(2)}, u32[]{:S(2)}) %collective-permute-start.3) | collective-permute-done | bytes 147488 | tf_op jit(solution)/shard_map/ppermute | solution.py:28
  23.3 0.7 %broadcast_select_fusion.4 = (bf16[2,8,2,768]{3,2,1,0:T(2,128)(2,1)}, bf16[2,8,2,768]{3,2,1,0:T(2,128)(2,1)S(1)}, bf16[2,8,2,768]{3,2,1,0:T(2,128)(2,1)S(1)}) fusion(pred[]{:T(512)S(6)} %eq.24, bf16[2,2,2,768]{3,2,1,0:T(2,128)(2,1)S(1)} %get-tuple-element.23, bf16[2,4,24,128]{3,2,1,0:T(8,128)(2,1)S(1)} %get-tuple-element.22, ...), kind=kLoop, calls=%fused_computation.6 | loop fusion | flops 516096 | bytes 491521 | tf_op jit(solution)/shard_map/jit(_where)/select_n | solution.py:26
  24.1 0.6 %broadcast_select_fusion.5 = bf16[2,2,8,768]{3,2,1,0:T(8,128)(2,1)} fusion(bf16[2,2,8,768]{3,2,1,0:T(8,128)(2,1)S(1)} %bitcast.20, bf16[2,2,8,768]{3,2,1,0:T(8,128)(2,1)S(1)} %bitcast.19, pred[]{:T(512)S(6)} %eq.24), kind=kLoop, calls=%fused_computation.7 | loop fusion | flops 24576 | bytes 147457 | tf_op jit(solution)/shard_map/jit(_where)/select_n | solution.py:25
  24.7 1.3 %collective-permute-start.4 = (bf16[2,8,2,768]{3,2,1,0:T(2,128)(2,1)}, bf16[2,8,2,768]{3,2,1,0:T(2,128)(2,1)}, u32[]{:S(2)}, u32[]{:S(2)}) collective-permute-start(bf16[2,8,2,768]{3,2,1,0:T(2,128)(2,1)} %bitcast.14), channel_id=1, source_target_pairs={{16,32},{32,16},{17,33},{33,17},{18,34},{34,18},{19,35},{35,19},{2... | collective-permute-start | bytes 147464 | tf_op jit(solution)/shard_map/ppermute | solution.py:27
  26.0 6.4 %collective-permute-start.5 = (bf16[2,8,2,768]{3,2,1,0:T(2,128)(2,1)}, bf16[2,8,2,768]{3,2,1,0:T(2,128)(2,1)}, u32[]{:S(2)}, u32[]{:S(2)}) collective-permute-start(bf16[2,8,2,768]{3,2,1,0:T(2,128)(2,1)} %get-tuple-element.8), channel_id=1, source_target_pairs={{0,16},{32,48},{16,0},{48,32},{1,17},{33,49},{17,1},{49,33},{2,18}... | collective-permute-start | bytes 147464 | tf_op jit(solution)/shard_map/ppermute | solution.py:28
  32.4 0.0 copy-start.2
  32.4 1.0 %copy-done.2 = bf16[3,3,3,64,64]{4,3,2,1,0:T(8,128)(2,1)S(1)} copy-done((bf16[3,3,3,64,64]{4,3,2,1,0:T(8,128)(2,1)S(1)}, bf16[3,3,3,64,64]{4,3,2,1,0:T(8,128)(2,1)}, u32[]{:S(2)}) %copy-start.2) | copy-done | bytes 221208
  33.4 1.0 %copy-done.3 = bf16[3,3,3,64,64]{4,3,2,1,0:T(8,128)(2,1)S(1)} copy-done((bf16[3,3,3,64,64]{4,3,2,1,0:T(8,128)(2,1)S(1)}, bf16[3,3,3,64,64]{4,3,2,1,0:T(8,128)(2,1)}, u32[]{:S(2)}) %copy-start.3) | copy-done | bytes 221208
  34.4 1.3 %shard_map.77 = (bf16[3072,256]{1,0:T(8,128)(2,1)S(1)}, bf16[3072,256]{1,0:T(8,128)(2,1)S(1)}, f32[2,256]{1,0:T(2,128)S(1)}) custom-call(bf16[3,3,192,64]{3,2,1,0:T(8,128)(2,1)S(1)} %bitcast.15, bf16[3,3,192,64]{3,2,1,0:T(8,128)(2,1)S(1)} %bitcast.16, f32[1,64]{1,0:T(1,128)S(1)} %bitcast.17, f32[1,64]{1,0:T(1,128)S(1)} %bitcast.18), custom_call_target="tpu_custom_call" | custom-call | tf_op jit(solution)/shard_map/pallas_call | solution.py:212
  35.8 0.1 stack.48.place
  35.9 0.8 %copy-done.5 = bf16[2,4,24,128]{3,2,1,0:T(8,128)(2,1)S(1)} copy-done((bf16[2,4,24,128]{3,2,1,0:T(8,128)(2,1)S(1)}, bf16[2,4,24,128]{3,2,1,0:T(8,128)(2,1)}, u32[]{:S(2)}) %copy-start.5) | copy-done | bytes 49176
  36.7 1.8 %shard_map.78.acc.mid = f32[3,320,256]{2,1,0:T(8,128)S(1)} custom-call(s32[9]{0:T(128)S(1)} %stack.48.place, bf16[2,4,24,512]{3,2,1,0:T(8,128)(2,1)S(1)} %pad_maximum_fusion.1.own, bf16[2,4,24,128]{3,2,1,0:T(8,128)(2,1)S(1)} %collective-permute-done.zf, bf16[2,4,24,128]{3,2,1,0:T(8,128)(2,1)S(1)} %copy-done.5, bf16[3072,256]{1,0:T(8,128)(2,1)S(1)} %get-tuple-element.5.wa), custom_call_target="tpu_custom_call" | custom-call | tf_op jit(solution)/shard_map/pallas_call | solution.py:212
  38.5 1.3 %shard_map.79.ends = f32[2,320,256]{2,1,0:T(8,128)S(1)} custom-call(s32[9]{0:T(128)S(1)} %stack.48.place, bf16[2,2,24,768]{3,2,1,0:T(8,128)(2,1)S(1)} %collective-permute-done.2.xf, bf16[2,2,24,768]{3,2,1,0:T(8,128)(2,1)S(1)} %copy-done.1, bf16[3072,256]{1,0:T(8,128)(2,1)S(1)} %get-tuple-element.5.wa, f32[3,320,256]{2,1,0:T(8,128)S(1)} %shard_map.78.acc.mid), custom_call_target="tpu_custom_call" | custom-call | tf_op jit(solution)/shard_map/pallas_call | solution.py:212
  39.8 0.0 collective-permute-done.4.yf
  39.8 3.9 %shard_map.80 = (bf16[4,24,512]{2,1,0:T(8,128)(2,1)}, bf16[4,24,512]{2,1,0:T(8,128)(2,1)}) custom-call(s32[9]{0:T(128)S(1)} %stack.48.place, bf16[2,8,2,768]{3,2,1,0:T(2,128)(2,1)} %collective-permute-done.4.yf, bf16[2,8,2,768]{3,2,1,0:T(2,128)(2,1)} %collective-permute-done.5.yn, f32[3,320,256]{2,1,0:T(8,128)S(1)} %shard_map.78.acc.mid, ...), custom_call_target="tpu_custom_call" | custom-call | tf_op jit(solution)/shard_map/pallas_call | solution.py:212
  (18 shorter events, 0.2 us)
Async XLA Ops:
  1.6 30.8 %copy-start.6 = (f32[64]{0:T(128)S(1)}, f32[64]{0:T(128)}, u32[]{:S(2)}) copy-start(f32[64]{0:T(128)} %param.9) | copy-start | bytes 772
  1.6 30.8 %copy-start.7 = (f32[64]{0:T(128)S(1)}, f32[64]{0:T(128)}, u32[]{:S(2)}) copy-start(f32[64]{0:T(128)} %param.11) | copy-start | bytes 772
  1.7 12.5 %collective-permute-start = (bf16[2,4,24,128]{3,2,1,0:T(8,128)(2,1)S(1)}, bf16[2,4,24,128]{3,2,1,0:T(8,128)(2,1)S(1)}, u32[]{:S(2)}, u32[]{:S(2)}) collective-permute-start(bf16[2,4,24,128]{3,2,1,0:T(8,128)(2,1)S(1)} %get-tuple-element.15), channel_id=1, source_target_pairs={{1,2},{3,4},{5,6},{7,8},{9,10},{11,12},{13,14},{2,1},{4,3},{6,5},{... | collective-permute-start | bytes 147464 | tf_op jit(solution)/shard_map/ppermute | solution.py:27
  10.7 6.0 %collective-permute-start.1 = (bf16[2,4,24,128]{3,2,1,0:T(8,128)(2,1)S(1)}, bf16[2,4,24,128]{3,2,1,0:T(8,128)(2,1)S(1)}, u32[]{:S(2)}, u32[]{:S(2)}) collective-permute-start(bf16[2,4,24,128]{3,2,1,0:T(8,128)(2,1)S(1)} %get-tuple-element.16), channel_id=1, source_target_pairs={{0,1},{2,3},{4,5},{6,7},{8,9},{10,11},{12,13},{14,15},{1,0},{3,2},... | collective-permute-start | bytes 147464 | tf_op jit(solution)/shard_map/ppermute | solution.py:28
  16.7 0.8 %copy-start.4 = (bf16[2,4,24,128]{3,2,1,0:T(8,128)(2,1)}, bf16[2,4,24,128]{3,2,1,0:T(8,128)(2,1)S(1)}, u32[]{:S(2)}) copy-start(bf16[2,4,24,128]{3,2,1,0:T(8,128)(2,1)S(1)} %collective-permute-done.1.zn) | copy-start | bytes 147460
  16.7 5.6 %collective-permute-start.2 = (bf16[2,2,24,768]{3,2,1,0:T(8,128)(2,1)S(1)}, bf16[2,2,24,768]{3,2,1,0:T(8,128)(2,1)S(1)}, u32[]{:S(2)}, u32[]{:S(2)}) collective-permute-start(bf16[2,2,24,768]{3,2,1,0:T(8,128)(2,1)S(1)} %get-tuple-element.13), channel_id=1, source_target_pairs={{64,128},{192,256},{320,384},{128,64},{256,192},{384,320},{65,129}... | collective-permute-start | bytes 442376 | tf_op jit(solution)/shard_map/ppermute | solution.py:27
  17.4 5.8 %collective-permute-start.3 = (bf16[2,2,24,768]{3,2,1,0:T(8,128)(2,1)S(1)}, bf16[2,2,24,768]{3,2,1,0:T(8,128)(2,1)S(1)}, u32[]{:S(2)}, u32[]{:S(2)}) collective-permute-start(bf16[2,2,24,768]{3,2,1,0:T(8,128)(2,1)S(1)} %get-tuple-element.14), channel_id=1, source_target_pairs={{0,64},{128,192},{256,320},{384,448},{64,0},{192,128},{320,256},{4... | collective-permute-start | bytes 442376 | tf_op jit(solution)/shard_map/ppermute | solution.py:28
  23.3 9.1 %copy-start = (bf16[2,2,24,768]{3,2,1,0:T(8,128)(2,1)}, bf16[2,2,24,768]{3,2,1,0:T(8,128)(2,1)S(1)}, u32[]{:S(2)}) copy-start(bf16[2,2,24,768]{3,2,1,0:T(8,128)(2,1)S(1)} %collective-permute-done.3.xn) | copy-start | bytes 442372
  24.7 15.1 %collective-permute-start.4 = (bf16[2,8,2,768]{3,2,1,0:T(2,128)(2,1)}, bf16[2,8,2,768]{3,2,1,0:T(2,128)(2,1)}, u32[]{:S(2)}, u32[]{:S(2)}) collective-permute-start(bf16[2,8,2,768]{3,2,1,0:T(2,128)(2,1)} %bitcast.14), channel_id=1, source_target_pairs={{16,32},{32,16},{17,33},{33,17},{18,34},{34,18},{19,35},{35,19},{2... | collective-permute-start | bytes 147464 | tf_op jit(solution)/shard_map/ppermute | solution.py:27
  26.0 13.8 %collective-permute-start.5 = (bf16[2,8,2,768]{3,2,1,0:T(2,128)(2,1)}, bf16[2,8,2,768]{3,2,1,0:T(2,128)(2,1)}, u32[]{:S(2)}, u32[]{:S(2)}) collective-permute-start(bf16[2,8,2,768]{3,2,1,0:T(2,128)(2,1)} %get-tuple-element.8), channel_id=1, source_target_pairs={{0,16},{32,48},{16,0},{48,32},{1,17},{33,49},{17,1},{49,33},{2,18}... | collective-permute-start | bytes 147464 | tf_op jit(solution)/shard_map/ppermute | solution.py:28
  32.4 1.0 %copy-start.2 = (bf16[3,3,3,64,64]{4,3,2,1,0:T(8,128)(2,1)S(1)}, bf16[3,3,3,64,64]{4,3,2,1,0:T(8,128)(2,1)}, u32[]{:S(2)}) copy-start(bf16[3,3,3,64,64]{4,3,2,1,0:T(8,128)(2,1)} %param.8) | copy-start | bytes 663556
  33.4 1.0 %copy-start.3 = (bf16[3,3,3,64,64]{4,3,2,1,0:T(8,128)(2,1)S(1)}, bf16[3,3,3,64,64]{4,3,2,1,0:T(8,128)(2,1)}, u32[]{:S(2)}) copy-start(bf16[3,3,3,64,64]{4,3,2,1,0:T(8,128)(2,1)} %param.10) | copy-start | bytes 663556
  35.9 2.6 %copy-start.1 = (bf16[2,2,24,768]{3,2,1,0:T(8,128)(2,1)S(1)}, bf16[2,2,24,768]{3,2,1,0:T(8,128)(2,1)}, u32[]{:S(2)}) copy-start(bf16[2,2,24,768]{3,2,1,0:T(8,128)(2,1)} %copy-done) | copy-start | bytes 442372
  35.9 0.8 %copy-start.5 = (bf16[2,4,24,128]{3,2,1,0:T(8,128)(2,1)S(1)}, bf16[2,4,24,128]{3,2,1,0:T(8,128)(2,1)}, u32[]{:S(2)}) copy-start(bf16[2,4,24,128]{3,2,1,0:T(8,128)(2,1)} %copy-done.4) | copy-start | bytes 147460

commit v3 on v2

--- a/solution.py
+++ b/solution.py
@@ -11,7 +11,7 @@
 ROWS = 32
 VM = pl.BlockSpec(memory_space=pltpu.VMEM)
 SM = pl.BlockSpec(memory_space=pltpu.SMEM)
-HB = pl.BlockSpec(memory_space=pl.ANY)
+HB = pl.BlockSpec(memory_space=pltpu.HBM)
 
 
 def swap_pairs(axis, first):
@@ -39,26 +39,55 @@
     return jnp.where(even, a, b).astype(F32), jnp.where(even, b, a).astype(F32)
 
 
-def weight_kernel(first, second, bias_a, bias_b, out_a, out_b, bias_out, raw, sems):
+def weight_kernel(first, second, bias_a, bias_b, out_a, out_b, bias_out, raw, low, sems):
     copies = [
-        pltpu.make_async_copy(source, raw.at[n], sems.at[n])
-        for n, source in enumerate((first, second))
+        pltpu.make_async_copy(source, target, sems.at[n])
+        for n, (source, target) in enumerate(
+            (
+                (first, raw.at[0]),
+                (second, raw.at[1]),
+                (bias_a, low.at[0]),
+                (bias_b, low.at[1]),
+            )
+        )
     ]
     for copy in copies:
         copy.start()
-    for row, bias in enumerate((bias_a, bias_b)):
-        b = bias[...]
+    gap = jnp.zeros((64, 64), BF16)
+    for n, target in enumerate((out_a, out_b)):
+        copies[n].wait()
+        for tap in range(9):
+            w = raw[n, tap]
+            target[256 * tap : 256 * tap + 256, :] = jnp.concatenate(
+                [
+                    jnp.concatenate([w, gap], axis=0),
+                    jnp.concatenate([gap, w], axis=0),
+                ],
+                axis=1,
+            )
+    for row in range(2):
+        copies[2 + row].wait()
+        b = low[row]
         bias_out[row : row + 1, :] = jnp.concatenate([b, b, b, b], axis=1)
-    for n, target in enumerate((out_a, out_b)):
-        target[...] = jnp.zeros(target.shape, BF16)
-        copies[n].wait()
-        for dy in range(3):
-            for dx in range(3):
-                w = raw[n, dx, dy]
-                for k in range(2):
-                    base = ((dx + k) * 3 + dy) * 256
-                    target[base : base + 192, 128 * k : 128 * k + 64] = w
-                    target[base + 64 : base + 256, 128 * k + 64 : 128 * k + 128] = w
+
+
+def columns(weights, planes):
+    none = jnp.zeros((256, 128), BF16)
+
+    def tap(dx, dy):
+        if not 0 <= dx <= 2:
+            return none
+        at = 256 * (3 * dx + dy)
+        return weights[at : at + 256, :]
+
+    return jnp.concatenate(
+        [
+            jnp.concatenate([tap(j, dy), tap(j - 1, dy)], axis=1)
+            for j in planes
+            for dy in range(3)
+        ],
+        axis=0,
+    )
 
 
 def taps(read, starts, pairs):
@@ -85,7 +114,7 @@
             shifted[dy, x] = both.reshape(2 * ROWS, both.shape[2])
 
 
-def own_kernel(place, own, zf, zn, wa, acc, ext, shifted):
+def own_kernel(place, own, zf, zn, wa, mid, ends, ext, shifted):
     nx, ny, nz = own.shape[1:]
     zl, zr = pick(place[5] == 1, zf, zn)
     ext[:, :, 0:2, :] = jnp.zeros_like(ext[:, :, 0:2, :])
@@ -96,18 +125,18 @@
     shift_rows(ext, shifted)
     read = lambda dy, x, p: shifted[dy, x, :, 128 * p : 128 * p + 256]
     pairs = nz // 128 + 1
-    half = wa.shape[0] // 2
     size = pairs * 2 * ROWS
     last = nx // 2
-    low = dot(taps(read, [(2 * i, 2 * i + 1) for i in range(last)], pairs), wa[:half])
-    high = dot(taps(read, [(2 * i, 2 * i + 1) for i in range(last)], pairs), wa[half:])
-    acc[0] = high[:size]
+    inner = taps(read, [(2 * i, 2 * i + 1) for i in range(last)], pairs)
+    low = dot(inner, columns(wa, (0, 1)))
+    high = dot(inner, columns(wa, (2, 3)))
+    ends[0] = high[:size]
     for i in range(1, last):
-        acc[i] = high[i * size : i * size + size] + low[(i - 1) * size : i * size]
-    acc[last] = low[(last - 1) * size :]
-
-
-def side_kernel(place, xf, xn, wa, acc, out, ext, shifted):
+        mid[i - 1] = high[i * size : i * size + size] + low[(i - 1) * size : i * size]
+    ends[1] = low[(last - 1) * size :]
+
+
+def side_kernel(place, xf, xn, wa, ends, out, ext, shifted):
     ny = xf.shape[2]
     xl, xr = pick(place[3] == 1, xf, xn)
     ext[:, :, 0:2, :] = jnp.zeros_like(ext[:, :, 0:2, :])
@@ -117,9 +146,8 @@
     shift_rows(ext, shifted)
     read = lambda dy, x, p: shifted[dy, x, :, 128 * p : 128 * p + 256]
     pairs = ext.shape[3] // 128 - 1
-    half = wa.shape[0] // 2
-    out[0] = acc[0] + dot(taps(read, [(0, 1)], pairs), wa[:half])
-    out[1] = acc[acc.shape[0] - 1] + dot(taps(read, [(2, 3)], pairs), wa[half:])
+    out[0] = ends[0] + dot(taps(read, [(0, 1)], pairs), columns(wa, (0, 1)))
+    out[1] = ends[1] + dot(taps(read, [(2, 3)], pairs), columns(wa, (2, 3)))
 
 
 def silu_pair(pre, direction):
@@ -132,7 +160,6 @@
 ):
     nx, ny, nz = out.shape
     pairs = nz // 128
-    half = wa.shape[0] // 2
     yl, yr = pick(place[4] == 1, yf, yn)
     edge[...] = jnp.zeros_like(edge)
     edge[0, :, :, 0:2, :] = yl
@@ -147,14 +174,14 @@
     blocks = nx // 2 + 1
     low = taps(read_edge, [(2 * i, 2 * i + 1) for i in range(blocks)], pairs + 1)
     high = taps(read_edge, [(2 * i + 2, 2 * i + 3) for i in range(blocks)], pairs + 1)
-    extra = dot(low, wa[:half]) + dot(high, wa[half:])
+    extra = dot(low, columns(wa, (0, 1))) + dot(high, columns(wa, (2, 3)))
     for i in range(blocks):
         if i == 0:
             acc[i] = ends[0]
         elif i == blocks - 1:
             acc[i] = ends[1]
         else:
-            acc[i] = mid[i]
+            acc[i] = mid[i - 1]
         for g in range(2 * (pairs + 1)):
             at = (i * 2 * (pairs + 1) + g) * 8
             top = ROWS * g
@@ -195,7 +222,7 @@
     blocks = nx // 2
     low = taps(read, [(2 * i, 2 * i + 1) for i in range(blocks)], pairs)
     high = taps(read, [(2 * i + 2, 2 * i + 3) for i in range(blocks)], pairs)
-    total = dot(low, wb[:half]) + dot(high, wb[half:])
+    total = dot(low, columns(wb, (0, 1))) + dot(high, columns(wb, (2, 3)))
     b = bias[1:2, :]
     for i in range(blocks):
         for p in range(pairs):
@@ -231,12 +258,16 @@
     )
     wa, wb, bias = call(
         weight_kernel,
-        [HB, HB, VM, VM],
-        [((3072, 256), BF16), ((3072, 256), BF16), ((2, 256), F32)],
-        [pltpu.VMEM((2, 3, 3, 192, 64), BF16), pltpu.SemaphoreType.DMA((2,))],
+        [HB] * 4,
+        [((2304, 128), BF16), ((2304, 128), BF16), ((2, 256), F32)],
+        [
+            pltpu.VMEM((2, 9, 192, 64), BF16),
+            pltpu.VMEM((2, 1, 64), F32),
+            pltpu.SemaphoreType.DMA((4,)),
+        ],
         (
-            first_weight.reshape(3, 3, 192, 64),
-            second_weight.reshape(3, 3, 192, 64),
+            first_weight.reshape(9, 192, 64),
+            second_weight.reshape(9, 192, 64),
             first_bias.reshape(1, 64),
             second_bias.reshape(1, 64),
         ),
@@ -258,10 +289,10 @@
         pltpu.VMEM((2, 4, ROWS + 8, wide), F32),
         pltpu.VMEM((3, 4, 2 * ROWS, wide), BF16),
     ]
-    (mid,) = call(
+    mid, ends_own = call(
         own_kernel,
         [SM] + [VM] * 4,
-        [((blocks, size, 256), F32)],
+        [((blocks - 2, size, 256), F32), ((2, size, 256), F32)],
         [
             pltpu.VMEM((2, nx, ROWS + 8, wide), F32),
             pltpu.VMEM((3, nx, 2 * ROWS, wide), BF16),
@@ -273,7 +304,7 @@
         [SM] + [VM] * 4,
         [((2, size, 256), F32)],
         work,
-        (place, xf, xn, wa, mid),
+        (place, xf, xn, wa, ends_own),
     )
     block = ((nx, ny, nz), BF16)
     return tuple(

time: 44.1 us -> 39.7 us (0.900)
  local copies, waits for them, and re-layouts: 3.02 us -> 0.78 us
  other arithmetic: 2.42 us -> 1.19 us
  Pallas kernels: 8.24 us -> 7.34 us
    unnamed x16 -> x8, local copies, waits for them, and re-layouts: 2.88 us -> 0.65 us
    pallas_call x4, Pallas kernels: 8.24 us -> 7.34 us  [call(): pl.pallas_call(kernel, in_specs=ins, out_specs=[VM] * len(outs), out_shap...]
    select_n x1, other arithmetic: 0.73 us -> 0.11 us  [swap(): to_near = jnp.where(even, tail, head)]
    select_n x3, other arithmetic: 0.67 us -> 0.05 us  [swap(): to_far = jnp.where(even, head, tail)]
    ppermute x3, starting transfers between devices: 13.1 us -> 13.7 us  [swap(): near = lax.ppermute(to_near, axis, swap_pairs(axis, 0))]
    ppermute x3, starting transfers between devices: 11 us -> 10.5 us  [swap(): far = lax.ppermute(to_far, axis, swap_pairs(axis, 1))]
where the time goes in v3:
time: 39.7 us; the launch traced here: 39.4 us
  starting transfers between devices  24.2 us (61%)
  Pallas kernels  7.34 us (18%)
  waiting for transfers between devices  5.01 us (13%)
  other arithmetic  1.19 us (3%)
  between operations  0.87 us (2%)
  local copies, waits for them, and re-layouts  0.78 us (2%)
    ppermute x3, starting transfers between devices, swap(): near = lax.ppermute(to_near, axis, swap_pairs(axis, 0))  13.7 us
    ppermute x3, starting transfers between devices, swap(): far = lax.ppermute(to_far, axis, swap_pairs(axis, 1))  10.5 us
    pallas_call x4, Pallas kernels, call(): pl.pallas_call(kernel, in_specs=ins, out_specs=[VM] * len(outs), out_shap...  7.34 us
    ppermute x3, waiting for transfers between devices, swap(): near = lax.ppermute(to_near, axis, swap_pairs(axis, 0))  3.44 us
    ppermute x3, waiting for transfers between devices, swap(): far = lax.ppermute(to_far, axis, swap_pairs(axis, 1))  1.57 us
    another operation x1, other arithmetic, shards(): own = lax.optimization_barrier(jnp.stack([source, tangent]))  0.96 us
  transfers between devices with their start and end apart: 6, of which 3 were waited for; matrix products, arithmetic and copies ran while one was open for 0% of the time, Pallas kernels for 10%

profile of v3, /device:TPU:6, one launch (start us, length us, event | category | flops | bytes accessed | tf_op | source)
XLA Modules:
  0.0 39.4 jit_solution(1536877439484229250)
XLA Ops:
  0.6 1.0 %pad_maximum_fusion.1.own = bf16[2,4,24,512]{3,2,1,0:T(8,128)(2,1)S(1)} fusion(bf16[1,4,24,512]{3,2,1,0:T(8,128)(2,1)} %bitcast.21, bf16[1,4,24,512]{3,2,1,0:T(8,128)(2,1)} %bitcast.22), kind=kLoop, calls=%fused_computation.1 | loop fusion | flops 98304 | bytes 393216 | tf_op jit(solution)/shard_map/stack | solution.py:251
  1.6 9.0 %collective-permute-start = (bf16[2,4,24,128]{3,2,1,0:T(8,128)(2,1)S(1)}, bf16[2,4,24,128]{3,2,1,0:T(8,128)(2,1)S(1)}, u32[]{:S(2)}, u32[]{:S(2)}) collective-permute-start(bf16[2,4,24,128]{3,2,1,0:T(8,128)(2,1)S(1)} %get-tuple-element.19), channel_id=1, source_target_pairs={{1,2},{3,4},{5,6},{7,8},{9,10},{11,12},{13,14},{2,1},{4,3},{6,5},{... | collective-permute-start | bytes 147464 | tf_op jit(solution)/shard_map/ppermute | solution.py:27
  10.6 1.9 %collective-permute-start.1 = (bf16[2,4,24,128]{3,2,1,0:T(8,128)(2,1)S(1)}, bf16[2,4,24,128]{3,2,1,0:T(8,128)(2,1)S(1)}, u32[]{:S(2)}, u32[]{:S(2)}) collective-permute-start(bf16[2,4,24,128]{3,2,1,0:T(8,128)(2,1)S(1)} %get-tuple-element.20), channel_id=1, source_target_pairs={{0,1},{2,3},{4,5},{6,7},{8,9},{10,11},{12,13},{14,15},{1,0},{3,2},... | collective-permute-start | bytes 147464 | tf_op jit(solution)/shard_map/ppermute | solution.py:28
  12.6 1.6 %collective-permute-done.zf = bf16[2,4,24,128]{3,2,1,0:T(8,128)(2,1)S(1)} collective-permute-done((bf16[2,4,24,128]{3,2,1,0:T(8,128)(2,1)S(1)}, bf16[2,4,24,128]{3,2,1,0:T(8,128)(2,1)S(1)}, u32[]{:S(2)}, u32[]{:S(2)}) %collective-permute-start) | collective-permute-done | bytes 49184 | tf_op jit(solution)/shard_map/ppermute | solution.py:27
  14.2 2.5 %collective-permute-done.1.zn = bf16[2,4,24,128]{3,2,1,0:T(8,128)(2,1)S(1)} collective-permute-done((bf16[2,4,24,128]{3,2,1,0:T(8,128)(2,1)S(1)}, bf16[2,4,24,128]{3,2,1,0:T(8,128)(2,1)S(1)}, u32[]{:S(2)}, u32[]{:S(2)}) %collective-permute-start.1) | collective-permute-done | bytes 49184 | tf_op jit(solution)/shard_map/ppermute | solution.py:28
  16.7 0.7 %collective-permute-start.2 = (bf16[2,2,24,768]{3,2,1,0:T(8,128)(2,1)S(1)}, bf16[2,2,24,768]{3,2,1,0:T(8,128)(2,1)S(1)}, u32[]{:S(2)}, u32[]{:S(2)}) collective-permute-start(bf16[2,2,24,768]{3,2,1,0:T(8,128)(2,1)S(1)} %get-tuple-element.17), channel_id=1, source_target_pairs={{64,128},{192,256},{320,384},{128,64},{256,192},{384,320},{65,129}... | collective-permute-start | bytes 442376 | tf_op jit(solution)/shard_map/ppermute | solution.py:27
  17.4 4.8 %collective-permute-start.3 = (bf16[2,2,24,768]{3,2,1,0:T(8,128)(2,1)S(1)}, bf16[2,2,24,768]{3,2,1,0:T(8,128)(2,1)S(1)}, u32[]{:S(2)}, u32[]{:S(2)}) collective-permute-start(bf16[2,2,24,768]{3,2,1,0:T(8,128)(2,1)S(1)} %get-tuple-element.18), channel_id=1, source_target_pairs={{0,64},{128,192},{256,320},{384,448},{64,0},{192,128},{320,256},{4... | collective-permute-start | bytes 442376 | tf_op jit(solution)/shard_map/ppermute | solution.py:28
  22.3 0.0 collective-permute-done.2.xf
  22.3 1.0 %collective-permute-done.3.xn = bf16[2,2,24,768]{3,2,1,0:T(8,128)(2,1)S(1)} collective-permute-done((bf16[2,2,24,768]{3,2,1,0:T(8,128)(2,1)S(1)}, bf16[2,2,24,768]{3,2,1,0:T(8,128)(2,1)S(1)}, u32[]{:S(2)}, u32[]{:S(2)}) %collective-permute-start.3) | collective-permute-done | bytes 147488 | tf_op jit(solution)/shard_map/ppermute | solution.py:28
  23.3 0.0 copy-start
  23.3 0.1 broadcast_select_fusion.4
  23.5 0.8 %collective-permute-start.4 = (bf16[2,8,2,768]{3,2,1,0:T(2,128)(2,1)S(1)}, bf16[2,8,2,768]{3,2,1,0:T(2,128)(2,1)S(1)}, u32[]{:S(2)}, u32[]{:S(2)}) collective-permute-start(bf16[2,8,2,768]{3,2,1,0:T(2,128)(2,1)S(1)} %bitcast.23), channel_id=1, source_target_pairs={{16,32},{32,16},{17,33},{33,17},{18,34},{34,18},{19,35},{35,19},{2... | collective-permute-start | bytes 147464 | tf_op jit(solution)/shard_map/ppermute | solution.py:27
  24.3 7.0 %collective-permute-start.5 = (bf16[2,8,2,768]{3,2,1,0:T(2,128)(2,1)S(1)}, bf16[2,8,2,768]{3,2,1,0:T(2,128)(2,1)S(1)}, u32[]{:S(2)}, u32[]{:S(2)}) collective-permute-start(bf16[2,8,2,768]{3,2,1,0:T(2,128)(2,1)S(1)} %get-tuple-element.12), channel_id=1, source_target_pairs={{0,16},{32,48},{16,0},{48,32},{1,17},{33,49},{17,1},{49,33},{2,18}... | collective-permute-start | bytes 147464 | tf_op jit(solution)/shard_map/ppermute | solution.py:28
  31.3 0.0 copy-start.2
  31.3 0.0 copy-start.3
  31.3 0.6 %copy-done.2 = f32[64]{0:T(128)S(1)} copy-done((f32[64]{0:T(128)S(1)}, f32[64]{0:T(128)}, u32[]{:S(2)}) %copy-start.2) | copy-done | bytes 280
  31.9 0.0 copy-done.3
  31.9 1.1 %shard_map.77 = (bf16[2304,128]{1,0:T(8,128)(2,1)S(1)}, bf16[2304,128]{1,0:T(8,128)(2,1)S(1)}, f32[2,256]{1,0:T(2,128)S(1)}) custom-call(bf16[9,192,64]{2,1,0:T(8,128)(2,1)S(1)} %bitcast.15, bf16[9,192,64]{2,1,0:T(8,128)(2,1)S(1)} %bitcast.16, f32[1,64]{1,0:T(1,128)S(1)} %bitcast.17, f32[1,64]{1,0:T(1,128)S(1)} %bitcast.18), custom_call_target="tpu_custom_call" | custom-call | tf_op jit(solution)/shard_map/pallas_call | solution.py:239
  33.0 0.1 stack.48.place
  33.1 1.8 %shard_map.78 = (f32[1,320,256]{2,1,0:T(8,128)S(1)}, f32[2,320,256]{2,1,0:T(8,128)S(1)}) custom-call(s32[9]{0:T(128)S(1)} %stack.48.place, bf16[2,4,24,512]{3,2,1,0:T(8,128)(2,1)S(1)} %pad_maximum_fusion.1.own, bf16[2,4,24,128]{3,2,1,0:T(8,128)(2,1)S(1)} %collective-permute-done.zf, bf16[2,4,24,128]{3,2,1,0:T(8,128)(2,1)S(1)} %collective-permute-done.1.zn, ...), custom_call_target="tpu_custom_call" | custom-call | tf_op jit(solution)/shard_map/pallas_call | solution.py:239
  34.9 1.3 %shard_map.79.ends = f32[2,320,256]{2,1,0:T(8,128)S(1)} custom-call(s32[9]{0:T(128)S(1)} %stack.48.place, bf16[2,2,24,768]{3,2,1,0:T(8,128)(2,1)S(1)} %collective-permute-done.2.xf, bf16[2,2,24,768]{3,2,1,0:T(8,128)(2,1)S(1)} %collective-permute-done.3.xn, bf16[2304,128]{1,0:T(8,128)(2,1)S(1)} %get-tuple-element.7.wa, f32[2,320,256]{2,1,0:T(8,128)S(1)} %get-tuple-element.9.ends), custom_call_target="tpu_custom_call" | custom-call | tf_op jit(solution)/shard_map/pallas_call | solution.py:239
  36.1 0.0 collective-permute-done.4.yf
  36.2 0.0 collective-permute-done.5.yn
  36.2 3.2 %shard_map.80 = (bf16[4,24,512]{2,1,0:T(8,128)(2,1)}, bf16[4,24,512]{2,1,0:T(8,128)(2,1)}) custom-call(s32[9]{0:T(128)S(1)} %stack.48.place, bf16[2,8,2,768]{3,2,1,0:T(2,128)(2,1)S(1)} %collective-permute-done.4.yf, bf16[2,8,2,768]{3,2,1,0:T(2,128)(2,1)S(1)} %collective-permute-done.5.yn, f32[1,320,256]{2,1,0:T(8,128)S(1)} %get-tuple-element.8.mid, ...), custom_call_target="tpu_custom_call" | custom-call | tf_op jit(solution)/shard_map/pallas_call | solution.py:239
  (10 shorter events, 0.2 us)
Async XLA Ops:
  1.6 12.5 %collective-permute-start = (bf16[2,4,24,128]{3,2,1,0:T(8,128)(2,1)S(1)}, bf16[2,4,24,128]{3,2,1,0:T(8,128)(2,1)S(1)}, u32[]{:S(2)}, u32[]{:S(2)}) collective-permute-start(bf16[2,4,24,128]{3,2,1,0:T(8,128)(2,1)S(1)} %get-tuple-element.19), channel_id=1, source_target_pairs={{1,2},{3,4},{5,6},{7,8},{9,10},{11,12},{13,14},{2,1},{4,3},{6,5},{... | collective-permute-start | bytes 147464 | tf_op jit(solution)/shard_map/ppermute | solution.py:27
  10.6 6.0 %collective-permute-start.1 = (bf16[2,4,24,128]{3,2,1,0:T(8,128)(2,1)S(1)}, bf16[2,4,24,128]{3,2,1,0:T(8,128)(2,1)S(1)}, u32[]{:S(2)}, u32[]{:S(2)}) collective-permute-start(bf16[2,4,24,128]{3,2,1,0:T(8,128)(2,1)S(1)} %get-tuple-element.20), channel_id=1, source_target_pairs={{0,1},{2,3},{4,5},{6,7},{8,9},{10,11},{12,13},{14,15},{1,0},{3,2},... | collective-permute-start | bytes 147464 | tf_op jit(solution)/shard_map/ppermute | solution.py:28
  16.7 5.5 %collective-permute-start.2 = (bf16[2,2,24,768]{3,2,1,0:T(8,128)(2,1)S(1)}, bf16[2,2,24,768]{3,2,1,0:T(8,128)(2,1)S(1)}, u32[]{:S(2)}, u32[]{:S(2)}) collective-permute-start(bf16[2,2,24,768]{3,2,1,0:T(8,128)(2,1)S(1)} %get-tuple-element.17), channel_id=1, source_target_pairs={{64,128},{192,256},{320,384},{128,64},{256,192},{384,320},{65,129}... | collective-permute-start | bytes 442376 | tf_op jit(solution)/shard_map/ppermute | solution.py:27
  17.4 5.8 %collective-permute-start.3 = (bf16[2,2,24,768]{3,2,1,0:T(8,128)(2,1)S(1)}, bf16[2,2,24,768]{3,2,1,0:T(8,128)(2,1)S(1)}, u32[]{:S(2)}, u32[]{:S(2)}) collective-permute-start(bf16[2,2,24,768]{3,2,1,0:T(8,128)(2,1)S(1)} %get-tuple-element.18), channel_id=1, source_target_pairs={{0,64},{128,192},{256,320},{384,448},{64,0},{192,128},{320,256},{4... | collective-permute-start | bytes 442376 | tf_op jit(solution)/shard_map/ppermute | solution.py:28
  23.2 8.1 %copy-start.1 = (bf16[3,3,3,64,64]{4,3,2,1,0:T(8,128)(2,1)S(1)}, bf16[3,3,3,64,64]{4,3,2,1,0:T(8,128)(2,1)}, u32[]{:S(2)}) copy-start(bf16[3,3,3,64,64]{4,3,2,1,0:T(8,128)(2,1)} %param.10) | copy-start | bytes 663556
  23.3 8.0 %copy-start = (bf16[3,3,3,64,64]{4,3,2,1,0:T(8,128)(2,1)S(1)}, bf16[3,3,3,64,64]{4,3,2,1,0:T(8,128)(2,1)}, u32[]{:S(2)}) copy-start(bf16[3,3,3,64,64]{4,3,2,1,0:T(8,128)(2,1)} %param.8) | copy-start | bytes 663556
  23.5 12.7 %collective-permute-start.4 = (bf16[2,8,2,768]{3,2,1,0:T(2,128)(2,1)S(1)}, bf16[2,8,2,768]{3,2,1,0:T(2,128)(2,1)S(1)}, u32[]{:S(2)}, u32[]{:S(2)}) collective-permute-start(bf16[2,8,2,768]{3,2,1,0:T(2,128)(2,1)S(1)} %bitcast.23), channel_id=1, source_target_pairs={{16,32},{32,16},{17,33},{33,17},{18,34},{34,18},{19,35},{35,19},{2... | collective-permute-start | bytes 147464 | tf_op jit(solution)/shard_map/ppermute | solution.py:27
  24.3 11.9 %collective-permute-start.5 = (bf16[2,8,2,768]{3,2,1,0:T(2,128)(2,1)S(1)}, bf16[2,8,2,768]{3,2,1,0:T(2,128)(2,1)S(1)}, u32[]{:S(2)}, u32[]{:S(2)}) collective-permute-start(bf16[2,8,2,768]{3,2,1,0:T(2,128)(2,1)S(1)} %get-tuple-element.12), channel_id=1, source_target_pairs={{0,16},{32,48},{16,0},{48,32},{1,17},{33,49},{17,1},{49,33},{2,18}... | collective-permute-start | bytes 147464 | tf_op jit(solution)/shard_map/ppermute | solution.py:28
  31.3 0.7 %copy-start.2 = (f32[64]{0:T(128)S(1)}, f32[64]{0:T(128)}, u32[]{:S(2)}) copy-start(f32[64]{0:T(128)} %param.9) | copy-start | bytes 772
  31.3 0.7 %copy-start.3 = (f32[64]{0:T(128)S(1)}, f32[64]{0:T(128)}, u32[]{:S(2)}) copy-start(f32[64]{0:T(128)} %param.11) | copy-start | bytes 772

commit v4 on v3

v4 whole, which is shorter than its diff:
```python
import functools

import jax
import jax.numpy as jnp
from jax import lax
from jax.experimental import pallas as pl
from jax.experimental.pallas import tpu as pltpu
from jax.sharding import PartitionSpec as P


F32 = jnp.float32
BF16 = jnp.bfloat16
ROWS = 32
VM = pl.BlockSpec(memory_space=pltpu.VMEM)
HB = pl.BlockSpec(memory_space=pltpu.HBM)


def both_ways(pairs):
    return pairs + [(j, i) for i, j in pairs]


def far_pairs(count):
    return [(i, i + 1) for i in range(1, count - 1, 2)]


def near_pairs(count):
    return [(i, i + 1) for i in range(0, count - 1, 2)]


def is_even(axis):
    return lax.axis_index(axis) % 2 == 0


def send(axis, operand, pairs):
    return lax.ppermute(operand, axis, both_ways(pairs))


def swap(axis, head, tail):
    even = is_even(axis)
    count = lax.axis_size(axis)
    far = send(axis, jnp.where(even, head, tail), far_pairs(count))
    near = send(axis, jnp.where(even, tail, head), near_pairs(count))
    return far, near


def sides(axis, far, near):
    even = is_even(axis)
    return jnp.where(even, far, near), jnp.where(even, near, far)


def pick(even, far, near):
    a, b = far[...], near[...]
    return jnp.where(even, a, b).astype(F32), jnp.where(even, b, a).astype(F32)


def late_near(count):
    group = 4
    middle = count // group // 2
    late = []
    for cut in range(group, count - 1, group):
        late.append((cut, cut + 1) if cut <= middle * group else (cut - 2, cut - 1))
    return late


def start_kernel(src, tan, first, second, bias_a, bias_b, own, far, near, raw_a, raw_b, low, sems):
    copies = [
        pltpu.make_async_copy(source, target, sems.at[n])
        for n, (source, target) in enumerate(
            (
                (src, own.at[0]),
                (tan, own.at[1]),
                (first, raw_a),
                (second, raw_b),
                (bias_a, low.at[0]),
                (bias_b, low.at[1]),
            )
        )
    ]
    for copy in copies:
        copy.start()
    even = is_even("gz")
    nz = own.shape[3]
    for f in range(2):
        copies[f].wait()
        head = own[f, :, :, 0:128]
        tail = own[f, :, :, nz - 128 :]
        far[f] = jnp.where(even, head, tail)
        near[f] = jnp.where(even, tail, head)
    for copy in copies[2:]:
        copy.wait()


def weight_kernel(raw_a, raw_b, low, out_a, out_b, bias_out):
    gap = jnp.zeros((64, 64), BF16)
    for raw, target in ((raw_a, out_a), (raw_b, out_b)):
        for tap in range(9):
            w = raw[tap]
            target[256 * tap : 256 * tap + 256, :] = jnp.concatenate(
                [
                    jnp.concatenate([w, gap], axis=0),
                    jnp.concatenate([gap, w], axis=0),
                ],
                axis=1,
            )
    for row in range(2):
        b = low[row]
        bias_out[row : row + 1, :] = jnp.concatenate([b, b, b, b], axis=1)


def columns(weights, planes):
    none = jnp.zeros((256, 128), BF16)

    def tap(dx, dy):
        if not 0 <= dx <= 2:
            return none
        at = 256 * (3 * dx + dy)
        return weights[at : at + 256, :]

    return jnp.concatenate(
        [
            jnp.concatenate([tap(j, dy), tap(j - 1, dy)], axis=1)
            for j in planes
            for dy in range(3)
        ],
        axis=0,
    )


def taps(read, starts, pairs):
    return jnp.concatenate(
        [
            jnp.concatenate(
                [read(dy, x, p) for x in planes for dy in range(3)], axis=1
            )
            for planes in starts
            for p in range(pairs)
        ],
        axis=0,
    )


def dot(lhs, rhs):
    return jnp.dot(lhs, rhs, preferred_element_type=F32)


def shift_rows(ext, shifted):
    for dy in range(3):
        for x in range(shifted.shape[1]):
            both = ext[:, x, dy : dy + ROWS, :].astype(BF16)
            shifted[dy, x] = both.reshape(2 * ROWS, both.shape[2])


def own_kernel(own, zl, zr, wa, mid, ends, ext, shifted):
    nx, ny, nz = own.shape[1:]
    ext[:, :, 0:2, :] = jnp.zeros_like(ext[:, :, 0:2, :])
    ext[:, :, 2 + ny :, :] = jnp.zeros_like(ext[:, :, 2 + ny :, :])
    ext[:, :, 2 : 2 + ny, 128 : 128 + nz] = own[...].astype(F32)
    ext[:, :, 2 : 2 + ny, 0:128] = zl[...].astype(F32)
    ext[:, :, 2 : 2 + ny, 128 + nz :] = zr[...].astype(F32)
    shift_rows(ext, shifted)
    read = lambda dy, x, p: shifted[dy, x, :, 128 * p : 128 * p + 256]
    pairs = nz // 128 + 1
    size = pairs * 2 * ROWS
    last = nx // 2
    inner = taps(read, [(2 * i, 2 * i + 1) for i in range(last)], pairs)
    low = dot(inner, columns(wa, (0, 1)))
    high = dot(inner, columns(wa, (2, 3)))
    ends[0] = high[:size]
    for i in range(1, last):
        mid[i - 1] = high[i * size : i * size + size] + low[(i - 1) * size : i * size]
    ends[1] = low[(last - 1) * size :]


def side_kernel(xl, xr, wa, ends, out, ext, shifted):
    ny = xl.shape[2]
    ext[:, :, 0:2, :] = jnp.zeros_like(ext[:, :, 0:2, :])
    ext[:, :, 2 + ny :, :] = jnp.zeros_like(ext[:, :, 2 + ny :, :])
    ext[:, 0:2, 2 : 2 + ny, :] = xl[...].astype(F32)
    ext[:, 2:4, 2 : 2 + ny, :] = xr[...].astype(F32)
    shift_rows(ext, shifted)
    read = lambda dy, x, p: shifted[dy, x, :, 128 * p : 128 * p + 256]
    pairs = ext.shape[3] // 128 - 1
    out[0] = ends[0] + dot(taps(read, [(0, 1)], pairs), columns(wa, (0, 1)))
    out[1] = ends[1] + dot(taps(read, [(2, 3)], pairs), columns(wa, (2, 3)))


def silu_pair(pre, direction):
    sig = jax.nn.sigmoid(pre)
    return pre * sig, sig * (1.0 + pre * (1.0 - sig)) * direction


def edge_rows(yl, yr, wa, edge, planes, pairs):
    for f in range(2):
        edge[:, 4 * f : 4 * f + 2, :] = yl[f]
        edge[:, 4 * f + 2 : 4 * f + 4, :] = yr[f]
    every = edge[...].reshape(edge.shape[0] * 8, edge.shape[2]).astype(BF16)
    lhs = jnp.concatenate(
        [every[:, 128 * p : 128 * p + 256] for p in range(pairs)], axis=0
    )
    taps_of = lambda dy: [wa[256 * (3 * dx + dy) : 256 * (3 * dx + dy) + 256, :] for dx in range(3)]
    order = taps_of(0) + taps_of(1) + taps_of(2)
    parts = [
        dot(lhs, jnp.concatenate(order[:4], axis=1)),
        dot(lhs, jnp.concatenate(order[4:], axis=1)),
    ]

    def tile(x, p, n):
        at = (p * edge.shape[0] + x) * 8
        part, column = (parts[0], n) if n < 4 else (parts[1], n - 4)
        return part[at : at + 8, 128 * column : 128 * column + 128]

    row = lax.broadcasted_iota(jnp.int32, (8, 128), 0) % 4
    out = {}
    for i in range(planes):
        for p in range(pairs):
            a, b, c = (
                tile(i, p, 3 * dy) + tile(i + 1, p, 3 * dy + 1) + tile(i + 2, p, 3 * dy + 2)
                for dy in range(3)
            )
            above = jnp.where(row == 0, pltpu.roll(b, 7, 0), 0.0)
            below = jnp.where(row == 3, pltpu.roll(b, 1, 0), 0.0)
            out[i, p] = jnp.where(row < 2, a + above, c + below)
    return out


def last_kernel(yf, yn, mid, ends, wa, wb, bias, out, out_t, edge, hid, shifted):
    nx, ny, nz = out.shape
    pairs = nz // 128
    yl, yr = pick(is_even("gy"), yf, yn)
    extra = edge_rows(yl, yr, wa, edge, nx + 2, pairs + 1)

    def limit(axis, low, high):
        at = lax.axis_index(axis)
        return (
            jnp.where(at == 0, low, -1),
            jnp.where(at == lax.axis_size(axis) - 1, high, -1),
        )

    x_low, x_high = limit("gx", 0, nx + 1)
    y_low, y_high = limit("gy", 0, ny + 1)
    z_low, z_high = limit("gz", 0, 1)
    rows = lax.broadcasted_iota(jnp.int32, (ROWS, 128), 0)
    halves = lax.broadcasted_iota(jnp.int32, (ROWS, 128), 1) // 64
    by_row = (rows == y_low) | (rows == y_high)
    first = by_row | (halves == z_low)
    final = by_row | (halves == z_high)
    first_row = lax.broadcasted_iota(jnp.int32, (8, 128), 0) < 2
    b = bias[0:1, 0:128]
    for i in range(nx + 2):
        k = 128 * (i % 2)
        if i < 2:
            source = ends.at[0]
        elif i >= nx:
            source = ends.at[1]
        else:
            source = mid.at[i // 2 - 1]
        for p in range(pairs + 1):
            fields = []
            for f in range(2):
                at = (2 * p + f) * ROWS
                e = extra[i, p]
                up = pltpu.roll(e, 4, 0) if f else e
                fields.append(
                    jnp.concatenate(
                        [
                            source[at : at + 8, k : k + 128] + jnp.where(first_row, up, 0.0),
                            source[at + 8 : at + ny, k : k + 128],
                            source[at + ny : at + ROWS, k : k + 128]
                            + jnp.where(first_row, pltpu.roll(e, 2 if f else 6, 0), 0.0),
                        ],
                        axis=0,
                    )
                )
            outside = first if p == 0 else final if p == pairs else by_row
            if i == 0:
                outside = outside | (rows * 0 == x_low)
            if i == nx + 1:
                outside = outside | (rows * 0 + nx + 1 == x_high)
            for f, value in enumerate(silu_pair(fields[0] + b, fields[1])):
                hid[f, i, 0:ROWS, 128 * p : 128 * p + 128] = jnp.where(outside, 0.0, value)

    for dy in range(3):
        for x in range(nx + 2):
            both = jnp.concatenate([hid[f, x, dy : dy + ny, :] for f in range(2)], axis=0)
            shifted[dy, x] = both.astype(BF16)
    read = lambda dy, x, p: shifted[dy, x, :, 128 * p : 128 * p + 256]
    blocks = nx // 2
    low = taps(read, [(2 * i, 2 * i + 1) for i in range(blocks)], pairs)
    high = taps(read, [(2 * i + 2, 2 * i + 3) for i in range(blocks)], pairs)
    total = dot(low, columns(wb, (0, 1))) + dot(high, columns(wb, (2, 3)))
    b = bias[1:2, :]
    for i in range(blocks):
        for p in range(pairs):
            at = (i * pairs + p) * 2 * ny
            value = silu_pair(total[at : at + ny] + b, total[at + ny : at + 2 * ny])
            for target, part in zip((out, out_t), value):
                for k in range(2):
                    target[2 * i + k, :, 128 * p : 128 * p + 128] = part[
                        :, 128 * k : 128 * k + 128
                    ].astype(BF16)


def call(kernel, ins, outs, scratch, args, mib=24):
    return pl.pallas_call(
        kernel,
        in_specs=ins,
        out_specs=[VM] * len(outs),
        out_shape=[jax.ShapeDtypeStruct(*o) for o in outs],
        scratch_shapes=scratch,
        compiler_params=pltpu.CompilerParams(vmem_limit_bytes=mib << 20),
    )(*args)


def shards(source, tangent, first_weight, first_bias, second_weight, second_bias):
    nx, ny, nz = source.shape
    raw = ((9, 192, 64), BF16)
    tail = ((2, nx, ny, 128), BF16)
    hbm = lambda x: pltpu.with_memory_space_constraint(x, pltpu.HBM)
    own, to_far, to_near, raw_a, raw_b, low = call(
        start_kernel,
        [HB] * 6,
        [((2, nx, ny, nz), BF16), tail, tail, raw, raw, ((2, 1, 64), F32)],
        [pltpu.SemaphoreType.DMA((6,))],
        tuple(
            hbm(x)
            for x in (
                source,
                tangent,
                first_weight.reshape(9, 192, 64),
                second_weight.reshape(9, 192, 64),
                first_bias.reshape(1, 64),
                second_bias.reshape(1, 64),
            )
        ),
    )
    tap = ((2304, 128), BF16)
    wa, wb, bias = call(
        weight_kernel, [VM] * 3, [tap, tap, ((2, 256), F32)], [], (raw_a, raw_b, low)
    )
    count = lax.axis_size("gz")
    late = late_near(count)
    early = [pair for pair in near_pairs(count) if pair not in late]
    z_early = send("gz", to_near, early)
    zf = send("gz", to_far, far_pairs(count))
    z_late = send("gz", to_near, late)
    at = lax.axis_index("gz")
    is_late = functools.reduce(jnp.logical_or, [at // 2 == pair[0] // 2 for pair in late])
    zl, zr = sides("gz", zf, jnp.where(is_late, z_late, z_early))
    ext = jnp.concatenate([zl, own, zr], axis=3)
    xl, xr = sides("gx", *swap("gx", ext[:, :2], ext[:, nx - 2 :]))
    ends = lambda at: jnp.concatenate(
        [part[:, :, at : at + 2] for part in (xl, ext, xr)], axis=1
    )
    yf, yn = swap("gy", ends(0), ends(ny - 2))

    wide = nz + 256
    blocks = nx // 2 + 1
    size = (nz // 128 + 1) * 2 * ROWS
    work = lambda planes: [
        pltpu.VMEM((2, planes, ROWS + 8, wide), F32),
        pltpu.VMEM((3, planes, 2 * ROWS, wide), BF16),
    ]
    mid, ends_own = call(
        own_kernel,
        [VM] * 4,
        [((blocks - 2, size, 256), F32), ((2, size, 256), F32)],
        work(nx),
        (own, zl, zr, wa),
    )
    (outer,) = call(side_kernel, [VM] * 4, [((2, size, 256), F32)], work(4), (xl, xr, wa, ends_own))
    block = ((nx, ny, nz), BF16)
    return tuple(
        call(
            last_kernel,
            [VM] * 7,
            [block, block],
            [
                pltpu.VMEM((nx + 4, 8, wide), F32),
                pltpu.VMEM((2, nx + 2, ROWS + 8, nz + 128), F32),
                pltpu.VMEM((3, nx + 2, 2 * ny, nz + 128), BF16),
            ],
            (yf, yn, mid, outer, wa, wb, bias),
        )
    )


def solution(mesh):
    return jax.shard_map(
        shards,
        mesh=mesh,
        in_specs=(P("gx", "gy", "gz"), P("gx", "gy", "gz"), P(), P(), P(), P()),
        out_specs=(P("gx", "gy", "gz"), P("gx", "gy", "gz")),
        check_vma=False,
    )
```

time: 39.7 us -> 36.1 us (0.909)
  the two profiles are of different devices: /device:TPU:6 before, /device:TPU:15 now
where the time goes in v4:
time: 36.1 us; the launch traced here: 35.8 us
  starting transfers between devices  25.5 us (71%)
  Pallas kernels  5.7 us (16%)
  waiting for transfers between devices  3.52 us (10%)
  between operations  0.84 us (2%)
    ppermute x7, starting transfers between devices, send(): return lax.ppermute(operand, axis, both_ways(pairs))  25.5 us
    pallas_call x5, Pallas kernels, call(): pl.pallas_call(kernel, in_specs=ins, out_specs=[VM] * len(outs), out_shap...  5.7 us
    ppermute x7, waiting for transfers between devices, send(): return lax.ppermute(operand, axis, both_ways(pairs))  3.52 us
  transfers between devices with their start and end apart: 7, of which 3 were waited for; matrix products, arithmetic and copies ran while one was open for 0% of the time, Pallas kernels for 6%

profile of v4, /device:TPU:15, one launch (start us, length us, event | category | flops | bytes accessed | tf_op | source)
XLA Modules:
  0.0 35.8 jit_solution(7248707968727462667)
XLA Ops:
  0.6 1.3 %shard_map.77 = (bf16[2,4,24,512]{3,2,1,0:T(8,128)(2,1)S(1)}, bf16[2,4,24,128]{3,2,1,0:T(8,128)(2,1)S(1)}, bf16[2,4,24,128]{3,2,1,0:T(8,128)(2,1)S(1)}, bf16[9,1...) custom-call(bf16[4,24,512]{2,1,0:T(8,128)(2,1)} %src.1, ...), custom_call_target="tpu_custom_call" | custom-call | tf_op jit(solution)/shard_map/pallas_call | solution.py:304
  1.9 8.7 %collective-permute-start = (bf16[2,4,24,128]{3,2,1,0:T(8,128)(2,1)S(1)}, bf16[2,4,24,128]{3,2,1,0:T(8,128)(2,1)S(1)}, u32[]{:S(2)}, u32[]{:S(2)}) collective-permute-start(bf16[2,4,24,128]{3,2,1,0:T(8,128)(2,1)S(1)} %get-tuple-element.13), channel_id=1, source_target_pairs={{1,2},{3,4},{5,6},{7,8},{9,10},{11,12},{13,14},{2,1},{4,3},{6,5},{... | collective-permute-start | bytes 147464 | tf_op jit(solution)/shard_map/ppermute | solution.py:35
  10.7 1.9 %collective-permute-start.2 = (bf16[2,4,24,128]{3,2,1,0:T(8,128)(2,1)S(1)}, bf16[2,4,24,128]{3,2,1,0:T(8,128)(2,1)S(1)}, u32[]{:S(2)}, u32[]{:S(2)}) collective-permute-start(bf16[2,4,24,128]{3,2,1,0:T(8,128)(2,1)S(1)} %get-tuple-element.14), channel_id=1, source_target_pairs={{0,1},{2,3},{6,7},{12,13},{14,15},{1,0},{3,2},{7,6},{13,12},{15,14... | collective-permute-start | bytes 147464 | tf_op jit(solution)/shard_map/ppermute | solution.py:35
  12.6 0.7 %collective-permute-start.1 = (bf16[2,4,24,128]{3,2,1,0:T(8,128)(2,1)S(1)}, bf16[2,4,24,128]{3,2,1,0:T(8,128)(2,1)S(1)}, u32[]{:S(2)}, u32[]{:S(2)}) collective-permute-start(bf16[2,4,24,128]{3,2,1,0:T(8,128)(2,1)S(1)} %get-tuple-element.14), channel_id=1, source_target_pairs={{4,5},{8,9},{10,11},{5,4},{9,8},{11,10},{20,21},{24,25},{26,27},{2... | collective-permute-start | bytes 147464 | tf_op jit(solution)/shard_map/ppermute | solution.py:35
  13.3 0.0 collective-permute-done
  13.3 2.2 %collective-permute-done.2 = bf16[2,4,24,128]{3,2,1,0:T(8,128)(2,1)S(1)} collective-permute-done((bf16[2,4,24,128]{3,2,1,0:T(8,128)(2,1)S(1)}, bf16[2,4,24,128]{3,2,1,0:T(8,128)(2,1)S(1)}, u32[]{:S(2)}, u32[]{:S(2)}) %collective-permute-start.2) | collective-permute-done | bytes 49184 | tf_op jit(solution)/shard_map/ppermute | solution.py:35
  15.5 0.0 collective-permute-done.1
  15.6 5.2 %collective-permute-start.3 = (bf16[2,2,24,768]{3,2,1,0:T(8,128)(2,1)S(1)}, bf16[2,2,24,768]{3,2,1,0:T(8,128)(2,1)S(1)}, u32[]{:S(2)}, u32[]{:S(2)}) collective-permute-start(bf16[2,2,24,768]{3,2,1,0:T(8,128)(2,1)S(1)} %get-tuple-element.29), channel_id=1, source_target_pairs={{64,128},{192,256},{320,384},{128,64},{256,192},{384,320},{65,129}... | collective-permute-start | bytes 442376 | tf_op jit(solution)/shard_map/ppermute | solution.py:35
  20.8 1.9 %collective-permute-start.4 = (bf16[2,2,24,768]{3,2,1,0:T(8,128)(2,1)S(1)}, bf16[2,2,24,768]{3,2,1,0:T(8,128)(2,1)S(1)}, u32[]{:S(2)}, u32[]{:S(2)}) collective-permute-start(bf16[2,2,24,768]{3,2,1,0:T(8,128)(2,1)S(1)} %get-tuple-element.30), channel_id=1, source_target_pairs={{0,64},{128,192},{256,320},{384,448},{64,0},{192,128},{320,256},{4... | collective-permute-start | bytes 442376 | tf_op jit(solution)/shard_map/ppermute | solution.py:35
  22.8 1.0 %collective-permute-done.3 = bf16[2,2,24,768]{3,2,1,0:T(8,128)(2,1)S(1)} collective-permute-done((bf16[2,2,24,768]{3,2,1,0:T(8,128)(2,1)S(1)}, bf16[2,2,24,768]{3,2,1,0:T(8,128)(2,1)S(1)}, u32[]{:S(2)}, u32[]{:S(2)}) %collective-permute-start.3) | collective-permute-done | bytes 147488 | tf_op jit(solution)/shard_map/ppermute | solution.py:35
  23.8 0.3 collective-permute-done.4
  24.2 0.1 broadcast_select_fusion.4
  24.3 0.7 %collective-permute-start.5 = (bf16[2,8,2,768]{3,2,1,0:T(2,128)(2,1)S(1)}, bf16[2,8,2,768]{3,2,1,0:T(2,128)(2,1)S(1)}, u32[]{:S(2)}, u32[]{:S(2)}) collective-permute-start(bf16[2,8,2,768]{3,2,1,0:T(2,128)(2,1)S(1)} %bitcast.11), channel_id=1, source_target_pairs={{16,32},{32,16},{17,33},{33,17},{18,34},{34,18},{19,35},{35,19},{2... | collective-permute-start | bytes 147464 | tf_op jit(solution)/shard_map/ppermute | solution.py:35
  25.0 6.4 %collective-permute-start.6 = (bf16[2,8,2,768]{3,2,1,0:T(2,128)(2,1)S(1)}, bf16[2,8,2,768]{3,2,1,0:T(2,128)(2,1)S(1)}, u32[]{:S(2)}, u32[]{:S(2)}) collective-permute-start(bf16[2,8,2,768]{3,2,1,0:T(2,128)(2,1)S(1)} %get-tuple-element.24), channel_id=1, source_target_pairs={{0,16},{32,48},{16,0},{48,32},{1,17},{33,49},{17,1},{49,33},{2,18}... | collective-permute-start | bytes 147464 | tf_op jit(solution)/shard_map/ppermute | solution.py:35
  31.4 0.3 shard_map.78
  31.7 1.2 %shard_map.79 = (f32[1,320,256]{2,1,0:T(8,128)S(1)}, f32[2,320,256]{2,1,0:T(8,128)S(1)}) custom-call(bf16[2,4,24,512]{3,2,1,0:T(8,128)(2,1)S(1)} %get-tuple-element.15.own, bf16[2,4,24,128]{3,2,1,0:T(8,128)(2,1)S(1)} %get-tuple-element.35.zl, bf16[2,4,24,128]{3,2,1,0:T(8,128)(2,1)S(1)} %get-tuple-element.36.zr, bf16[2304,128]{1,0:T(8,128)(2,1)S(1)} %get-tuple-element.19.wa), custom_call_target="tpu_custom_call" | custom-call | tf_op jit(solution)/shard_map/pallas_call | solution.py:304
  33.0 0.7 %shard_map.80.ends = f32[2,320,256]{2,1,0:T(8,128)S(1)} custom-call(bf16[2,2,24,768]{3,2,1,0:T(8,128)(2,1)S(1)} %get-tuple-element.27.xl, bf16[2,2,24,768]{3,2,1,0:T(8,128)(2,1)S(1)} %get-tuple-element.28.xr, bf16[2304,128]{1,0:T(8,128)(2,1)S(1)} %get-tuple-element.19.wa, f32[2,320,256]{2,1,0:T(8,128)S(1)} %get-tuple-element.21.ends), custom_call_target="tpu_custom_call" | custom-call | tf_op jit(solution)/shard_map/pallas_call | solution.py:304
  33.7 0.0 collective-permute-done.5.yf
  33.7 0.0 collective-permute-done.6.yn
  33.7 2.1 %shard_map.81 = (bf16[4,24,512]{2,1,0:T(8,128)(2,1)}, bf16[4,24,512]{2,1,0:T(8,128)(2,1)}) custom-call(bf16[2,8,2,768]{3,2,1,0:T(2,128)(2,1)S(1)} %collective-permute-done.5.yf, bf16[2,8,2,768]{3,2,1,0:T(2,128)(2,1)S(1)} %collective-permute-done.6.yn, f32[1,320,256]{2,1,0:T(8,128)S(1)} %get-tuple-element.20.mid, f32[2,320,256]{2,1,0:T(8,128)S(1)} %shard_map.80.ends, ...), custom_call_target="tpu_custom_call" | custom-call | tf_op jit(solution)/shard_map/pallas_call | solution.py:304
  (6 shorter events, 0.1 us)
Async XLA Ops:
  1.9 11.4 %collective-permute-start = (bf16[2,4,24,128]{3,2,1,0:T(8,128)(2,1)S(1)}, bf16[2,4,24,128]{3,2,1,0:T(8,128)(2,1)S(1)}, u32[]{:S(2)}, u32[]{:S(2)}) collective-permute-start(bf16[2,4,24,128]{3,2,1,0:T(8,128)(2,1)S(1)} %get-tuple-element.13), channel_id=1, source_target_pairs={{1,2},{3,4},{5,6},{7,8},{9,10},{11,12},{13,14},{2,1},{4,3},{6,5},{... | collective-permute-start | bytes 147464 | tf_op jit(solution)/shard_map/ppermute | solution.py:35
  10.7 4.8 %collective-permute-start.2 = (bf16[2,4,24,128]{3,2,1,0:T(8,128)(2,1)S(1)}, bf16[2,4,24,128]{3,2,1,0:T(8,128)(2,1)S(1)}, u32[]{:S(2)}, u32[]{:S(2)}) collective-permute-start(bf16[2,4,24,128]{3,2,1,0:T(8,128)(2,1)S(1)} %get-tuple-element.14), channel_id=1, source_target_pairs={{0,1},{2,3},{6,7},{12,13},{14,15},{1,0},{3,2},{7,6},{13,12},{15,14... | collective-permute-start | bytes 147464 | tf_op jit(solution)/shard_map/ppermute | solution.py:35
  12.6 2.9 %collective-permute-start.1 = (bf16[2,4,24,128]{3,2,1,0:T(8,128)(2,1)S(1)}, bf16[2,4,24,128]{3,2,1,0:T(8,128)(2,1)S(1)}, u32[]{:S(2)}, u32[]{:S(2)}) collective-permute-start(bf16[2,4,24,128]{3,2,1,0:T(8,128)(2,1)S(1)} %get-tuple-element.14), channel_id=1, source_target_pairs={{4,5},{8,9},{10,11},{5,4},{9,8},{11,10},{20,21},{24,25},{26,27},{2... | collective-permute-start | bytes 147464 | tf_op jit(solution)/shard_map/ppermute | solution.py:35
  15.6 8.2 %collective-permute-start.3 = (bf16[2,2,24,768]{3,2,1,0:T(8,128)(2,1)S(1)}, bf16[2,2,24,768]{3,2,1,0:T(8,128)(2,1)S(1)}, u32[]{:S(2)}, u32[]{:S(2)}) collective-permute-start(bf16[2,2,24,768]{3,2,1,0:T(8,128)(2,1)S(1)} %get-tuple-element.29), channel_id=1, source_target_pairs={{64,128},{192,256},{320,384},{128,64},{256,192},{384,320},{65,129}... | collective-permute-start | bytes 442376 | tf_op jit(solution)/shard_map/ppermute | solution.py:35
  20.8 3.3 %collective-permute-start.4 = (bf16[2,2,24,768]{3,2,1,0:T(8,128)(2,1)S(1)}, bf16[2,2,24,768]{3,2,1,0:T(8,128)(2,1)S(1)}, u32[]{:S(2)}, u32[]{:S(2)}) collective-permute-start(bf16[2,2,24,768]{3,2,1,0:T(8,128)(2,1)S(1)} %get-tuple-element.30), channel_id=1, source_target_pairs={{0,64},{128,192},{256,320},{384,448},{64,0},{192,128},{320,256},{4... | collective-permute-start | bytes 442376 | tf_op jit(solution)/shard_map/ppermute | solution.py:35
  24.3 9.4 %collective-permute-start.5 = (bf16[2,8,2,768]{3,2,1,0:T(2,128)(2,1)S(1)}, bf16[2,8,2,768]{3,2,1,0:T(2,128)(2,1)S(1)}, u32[]{:S(2)}, u32[]{:S(2)}) collective-permute-start(bf16[2,8,2,768]{3,2,1,0:T(2,128)(2,1)S(1)} %bitcast.11), channel_id=1, source_target_pairs={{16,32},{32,16},{17,33},{33,17},{18,34},{34,18},{19,35},{35,19},{2... | collective-permute-start | bytes 147464 | tf_op jit(solution)/shard_map/ppermute | solution.py:35
  25.0 8.8 %collective-permute-start.6 = (bf16[2,8,2,768]{3,2,1,0:T(2,128)(2,1)S(1)}, bf16[2,8,2,768]{3,2,1,0:T(2,128)(2,1)S(1)}, u32[]{:S(2)}, u32[]{:S(2)}) collective-permute-start(bf16[2,8,2,768]{3,2,1,0:T(2,128)(2,1)S(1)} %get-tuple-element.24), channel_id=1, source_target_pairs={{0,16},{32,48},{16,0},{48,32},{1,17},{33,49},{17,1},{49,33},{2,18}... | collective-permute-start | bytes 147464 | tf_op jit(solution)/shard_map/ppermute | solution.py:35

commit v5 on v4

--- a/solution.py
+++ b/solution.py
@@ -1,5 +1,3 @@
-import functools
-
 import jax
 import jax.numpy as jnp
 from jax import lax
@@ -35,12 +33,16 @@
     return lax.ppermute(operand, axis, both_ways(pairs))
 
 
+def exchange(axis, to_far, to_near):
+    count = lax.axis_size(axis)
+    far = send(axis, to_far, far_pairs(count))
+    near = send(axis, to_near, near_pairs(count))
+    return far, near
+
+
 def swap(axis, head, tail):
     even = is_even(axis)
-    count = lax.axis_size(axis)
-    far = send(axis, jnp.where(even, head, tail), far_pairs(count))
-    near = send(axis, jnp.where(even, tail, head), near_pairs(count))
-    return far, near
+    return exchange(axis, jnp.where(even, head, tail), jnp.where(even, tail, head))
 
 
 def sides(axis, far, near):
@@ -53,48 +55,45 @@
     return jnp.where(even, a, b).astype(F32), jnp.where(even, b, a).astype(F32)
 
 
-def late_near(count):
-    group = 4
-    middle = count // group // 2
-    late = []
-    for cut in range(group, count - 1, group):
-        late.append((cut, cut + 1) if cut <= middle * group else (cut - 2, cut - 1))
-    return late
-
-
-def start_kernel(src, tan, first, second, bias_a, bias_b, own, far, near, raw_a, raw_b, low, sems):
+def start_kernel(src, tan, far, near, sems):
+    even = is_even("gz")
+    tail = src.shape[2] - 128
+    copies = []
+    for f, field in enumerate((src, tan)):
+        for n, (target, at) in enumerate(
+            ((far, jnp.where(even, 0, tail)), (near, jnp.where(even, tail, 0)))
+        ):
+            part = field.at[:, :, pl.ds(pl.multiple_of(at, 128), 128)]
+            copies.append(pltpu.make_async_copy(part, target.at[f], sems.at[2 * f + n]))
+    for copy in copies:
+        copy.start()
+    for copy in copies:
+        copy.wait()
+
+
+def prep_kernel(
+    src, tan, first, second, bias_a, bias_b, own, out_a, out_b, bias_out, raw, low, sems
+):
     copies = [
         pltpu.make_async_copy(source, target, sems.at[n])
         for n, (source, target) in enumerate(
             (
+                (first, raw.at[0]),
+                (second, raw.at[1]),
+                (bias_a, low.at[0]),
+                (bias_b, low.at[1]),
                 (src, own.at[0]),
                 (tan, own.at[1]),
-                (first, raw_a),
-                (second, raw_b),
-                (bias_a, low.at[0]),
-                (bias_b, low.at[1]),
             )
         )
     ]
     for copy in copies:
         copy.start()
-    even = is_even("gz")
-    nz = own.shape[3]
-    for f in range(2):
-        copies[f].wait()
-        head = own[f, :, :, 0:128]
-        tail = own[f, :, :, nz - 128 :]
-        far[f] = jnp.where(even, head, tail)
-        near[f] = jnp.where(even, tail, head)
-    for copy in copies[2:]:
-        copy.wait()
-
-
-def weight_kernel(raw_a, raw_b, low, out_a, out_b, bias_out):
     gap = jnp.zeros((64, 64), BF16)
-    for raw, target in ((raw_a, out_a), (raw_b, out_b)):
+    for n, target in enumerate((out_a, out_b)):
+        copies[n].wait()
         for tap in range(9):
-            w = raw[tap]
+            w = raw[n, tap]
             target[256 * tap : 256 * tap + 256, :] = jnp.concatenate(
                 [
                     jnp.concatenate([w, gap], axis=0),
@@ -103,8 +102,11 @@
                 axis=1,
             )
     for row in range(2):
+        copies[2 + row].wait()
         b = low[row]
         bias_out[row : row + 1, :] = jnp.concatenate([b, b, b, b], axis=1)
+    for copy in copies[4:]:
+        copy.wait()
 
 
 def columns(weights, planes):
@@ -313,39 +315,31 @@
 
 def shards(source, tangent, first_weight, first_bias, second_weight, second_bias):
     nx, ny, nz = source.shape
-    raw = ((9, 192, 64), BF16)
     tail = ((2, nx, ny, 128), BF16)
     hbm = lambda x: pltpu.with_memory_space_constraint(x, pltpu.HBM)
-    own, to_far, to_near, raw_a, raw_b, low = call(
-        start_kernel,
+    fields = (hbm(source), hbm(tangent))
+    to_far, to_near = call(
+        start_kernel, [HB] * 2, [tail, tail], [pltpu.SemaphoreType.DMA((4,))], fields
+    )
+    tap = ((2304, 128), BF16)
+    own, wa, wb, bias = call(
+        prep_kernel,
         [HB] * 6,
-        [((2, nx, ny, nz), BF16), tail, tail, raw, raw, ((2, 1, 64), F32)],
-        [pltpu.SemaphoreType.DMA((6,))],
-        tuple(
-            hbm(x)
-            for x in (
-                source,
-                tangent,
-                first_weight.reshape(9, 192, 64),
-                second_weight.reshape(9, 192, 64),
-                first_bias.reshape(1, 64),
-                second_bias.reshape(1, 64),
-            )
+        [((2, nx, ny, nz), BF16), tap, tap, ((2, 256), F32)],
+        [
+            pltpu.VMEM((2, 9, 192, 64), BF16),
+            pltpu.VMEM((2, 1, 64), F32),
+            pltpu.SemaphoreType.DMA((6,)),
+        ],
+        fields
+        + (
+            hbm(first_weight.reshape(9, 192, 64)),
+            hbm(second_weight.reshape(9, 192, 64)),
+            hbm(first_bias.reshape(1, 64)),
+            hbm(second_bias.reshape(1, 64)),
         ),
     )
-    tap = ((2304, 128), BF16)
-    wa, wb, bias = call(
-        weight_kernel, [VM] * 3, [tap, tap, ((2, 256), F32)], [], (raw_a, raw_b, low)
-    )
-    count = lax.axis_size("gz")
-    late = late_near(count)
-    early = [pair for pair in near_pairs(count) if pair not in late]
-    z_early = send("gz", to_near, early)
-    zf = send("gz", to_far, far_pairs(count))
-    z_late = send("gz", to_near, late)
-    at = lax.axis_index("gz")
-    is_late = functools.reduce(jnp.logical_or, [at // 2 == pair[0] // 2 for pair in late])
-    zl, zr = sides("gz", zf, jnp.where(is_late, z_late, z_early))
+    zl, zr = sides("gz", *exchange("gz", to_far, to_near))
     ext = jnp.concatenate([zl, own, zr], axis=3)
     xl, xr = sides("gx", *swap("gx", ext[:, :2], ext[:, nx - 2 :]))
     ends = lambda at: jnp.concatenate(

time: 36.1 us -> 35.5 us (0.983)
  the two profiles are of different devices: /device:TPU:15 before, /device:TPU:38 now
where the time goes in v5:
time: 35.5 us; the launch traced here: 35.2 us
  starting transfers between devices  22.2 us (63%)
  Pallas kernels  6.47 us (18%)
  waiting for transfers between devices  5.47 us (15%)
  between operations  0.81 us (2%)
    ppermute x6, starting transfers between devices, send(): return lax.ppermute(operand, axis, both_ways(pairs))  22.2 us
    pallas_call x5, Pallas kernels, call(): pl.pallas_call(kernel, in_specs=ins, out_specs=[VM] * len(outs), out_shap...  6.47 us
    ppermute x6, waiting for transfers between devices, send(): return lax.ppermute(operand, axis, both_ways(pairs))  5.47 us
  transfers between devices with their start and end apart: 6, of which 3 were waited for; matrix products, arithmetic and copies ran while one was open for 0% of the time, Pallas kernels for 10%

profile of v5, /device:TPU:38, one launch (start us, length us, event | category | flops | bytes accessed | tf_op | source)
XLA Modules:
  0.0 35.2 jit_solution(1052446065077640343)
XLA Ops:
  0.6 0.9 %shard_map.77 = (bf16[2,4,24,128]{3,2,1,0:T(8,128)(2,1)S(1)}, bf16[2,4,24,128]{3,2,1,0:T(8,128)(2,1)S(1)}) custom-call(bf16[4,24,512]{2,1,0:T(8,128)(2,1)} %src.3, bf16[4,24,512]{2,1,0:T(8,128)(2,1)} %tan.3), custom_call_target="tpu_custom_call" | custom-call | tf_op jit(solution)/shard_map/pallas_call | solution.py:306
  1.5 9.0 %collective-permute-start = (bf16[2,4,24,128]{3,2,1,0:T(8,128)(2,1)S(1)}, bf16[2,4,24,128]{3,2,1,0:T(8,128)(2,1)S(1)}, u32[]{:S(2)}, u32[]{:S(2)}) collective-permute-start(bf16[2,4,24,128]{3,2,1,0:T(8,128)(2,1)S(1)} %get-tuple-element.10), channel_id=1, source_target_pairs={{1,2},{3,4},{5,6},{7,8},{9,10},{11,12},{13,14},{2,1},{4,3},{6,5},{... | collective-permute-start | bytes 147464 | tf_op jit(solution)/shard_map/ppermute | solution.py:33
  10.5 1.9 %collective-permute-start.1 = (bf16[2,4,24,128]{3,2,1,0:T(8,128)(2,1)S(1)}, bf16[2,4,24,128]{3,2,1,0:T(8,128)(2,1)S(1)}, u32[]{:S(2)}, u32[]{:S(2)}) collective-permute-start(bf16[2,4,24,128]{3,2,1,0:T(8,128)(2,1)S(1)} %get-tuple-element.11), channel_id=1, source_target_pairs={{0,1},{2,3},{4,5},{6,7},{8,9},{10,11},{12,13},{14,15},{1,0},{3,2},... | collective-permute-start | bytes 147464 | tf_op jit(solution)/shard_map/ppermute | solution.py:33
  12.5 1.6 %shard_map.78 = (bf16[2,4,24,512]{3,2,1,0:T(8,128)(2,1)S(1)}, bf16[2304,128]{1,0:T(8,128)(2,1)S(1)}, bf16[2304,128]{1,0:T(8,128)(2,1)S(1)}, f32[2,256]{1,0:T(2,128)S(1)}) custom-call(bf16[4,24,512]{2,1,0:T(8,128)(2,1)} %src.3, bf16[4,24,512]{2,1,0:T(8,128)(2,1)} %tan.3, bf16[9,192,64]{2,1,0:T(8,128)(2,1)} %bitcast.7, bf16[9,192,64]{2,1,0:T(8,128)(2,1)} %bitcast.8, ...), custom_call_target="tpu_custom_call" | custom-call | tf_op jit(solution)/shard_map/pallas_call | solution.py:306
  14.1 0.0 collective-permute-done
  14.1 2.4 %collective-permute-done.1 = bf16[2,4,24,128]{3,2,1,0:T(8,128)(2,1)S(1)} collective-permute-done((bf16[2,4,24,128]{3,2,1,0:T(8,128)(2,1)S(1)}, bf16[2,4,24,128]{3,2,1,0:T(8,128)(2,1)S(1)}, u32[]{:S(2)}, u32[]{:S(2)}) %collective-permute-start.1) | collective-permute-done | bytes 49184 | tf_op jit(solution)/shard_map/ppermute | solution.py:33
  16.6 0.7 %collective-permute-start.2 = (bf16[2,2,24,768]{3,2,1,0:T(8,128)(2,1)S(1)}, bf16[2,2,24,768]{3,2,1,0:T(8,128)(2,1)S(1)}, u32[]{:S(2)}, u32[]{:S(2)}) collective-permute-start(bf16[2,2,24,768]{3,2,1,0:T(8,128)(2,1)S(1)} %get-tuple-element.23), channel_id=1, source_target_pairs={{64,128},{192,256},{320,384},{128,64},{256,192},{384,320},{65,129}... | collective-permute-start | bytes 442376 | tf_op jit(solution)/shard_map/ppermute | solution.py:33
  17.3 4.8 %collective-permute-start.3 = (bf16[2,2,24,768]{3,2,1,0:T(8,128)(2,1)S(1)}, bf16[2,2,24,768]{3,2,1,0:T(8,128)(2,1)S(1)}, u32[]{:S(2)}, u32[]{:S(2)}) collective-permute-start(bf16[2,2,24,768]{3,2,1,0:T(8,128)(2,1)S(1)} %get-tuple-element.24), channel_id=1, source_target_pairs={{0,64},{128,192},{256,320},{384,448},{64,0},{192,128},{320,256},{4... | collective-permute-start | bytes 442376 | tf_op jit(solution)/shard_map/ppermute | solution.py:33
  22.1 0.0 collective-permute-done.2
  22.1 1.0 %collective-permute-done.3 = bf16[2,2,24,768]{3,2,1,0:T(8,128)(2,1)S(1)} collective-permute-done((bf16[2,2,24,768]{3,2,1,0:T(8,128)(2,1)S(1)}, bf16[2,2,24,768]{3,2,1,0:T(8,128)(2,1)S(1)}, u32[]{:S(2)}, u32[]{:S(2)}) %collective-permute-start.3) | collective-permute-done | bytes 147488 | tf_op jit(solution)/shard_map/ppermute | solution.py:33
  23.2 0.1 broadcast_select_fusion.4
  23.3 3.8 %collective-permute-start.4 = (bf16[2,8,2,768]{3,2,1,0:T(2,128)(2,1)S(1)}, bf16[2,8,2,768]{3,2,1,0:T(2,128)(2,1)S(1)}, u32[]{:S(2)}, u32[]{:S(2)}) collective-permute-start(bf16[2,8,2,768]{3,2,1,0:T(2,128)(2,1)S(1)} %bitcast.11), channel_id=1, source_target_pairs={{16,32},{32,16},{17,33},{33,17},{18,34},{34,18},{19,35},{35,19},{2... | collective-permute-start | bytes 147464 | tf_op jit(solution)/shard_map/ppermute | solution.py:33
  27.1 1.9 %collective-permute-start.5 = (bf16[2,8,2,768]{3,2,1,0:T(2,128)(2,1)S(1)}, bf16[2,8,2,768]{3,2,1,0:T(2,128)(2,1)S(1)}, u32[]{:S(2)}, u32[]{:S(2)}) collective-permute-start(bf16[2,8,2,768]{3,2,1,0:T(2,128)(2,1)S(1)} %get-tuple-element.18), channel_id=1, source_target_pairs={{0,16},{32,48},{16,0},{48,32},{1,17},{33,49},{17,1},{49,33},{2,18}... | collective-permute-start | bytes 147464 | tf_op jit(solution)/shard_map/ppermute | solution.py:33
  29.1 1.2 %shard_map.79 = (f32[1,320,256]{2,1,0:T(8,128)S(1)}, f32[2,320,256]{2,1,0:T(8,128)S(1)}) custom-call(bf16[2,4,24,512]{3,2,1,0:T(8,128)(2,1)S(1)} %get-tuple-element.12.own, bf16[2,4,24,128]{3,2,1,0:T(8,128)(2,1)S(1)} %get-tuple-element.29.zl, bf16[2,4,24,128]{3,2,1,0:T(8,128)(2,1)S(1)} %get-tuple-element.30.zr, bf16[2304,128]{1,0:T(8,128)(2,1)S(1)} %get-tuple-element.13.wa), custom_call_target="tpu_custom_call" | custom-call | tf_op jit(solution)/shard_map/pallas_call | solution.py:306
  30.3 0.7 %shard_map.80.ends = f32[2,320,256]{2,1,0:T(8,128)S(1)} custom-call(bf16[2,2,24,768]{3,2,1,0:T(8,128)(2,1)S(1)} %get-tuple-element.21.xl, bf16[2,2,24,768]{3,2,1,0:T(8,128)(2,1)S(1)} %get-tuple-element.22.xr, bf16[2304,128]{1,0:T(8,128)(2,1)S(1)} %get-tuple-element.13.wa, f32[2,320,256]{2,1,0:T(8,128)S(1)} %get-tuple-element.15.ends), custom_call_target="tpu_custom_call" | custom-call | tf_op jit(solution)/shard_map/pallas_call | solution.py:306
  31.0 0.0 collective-permute-done.4.yf
  31.0 2.1 %collective-permute-done.5.yn = bf16[2,8,2,768]{3,2,1,0:T(2,128)(2,1)S(1)} collective-permute-done((bf16[2,8,2,768]{3,2,1,0:T(2,128)(2,1)S(1)}, bf16[2,8,2,768]{3,2,1,0:T(2,128)(2,1)S(1)}, u32[]{:S(2)}, u32[]{:S(2)}) %collective-permute-start.5) | collective-permute-done | bytes 49184 | tf_op jit(solution)/shard_map/ppermute | solution.py:33
  33.1 2.1 %shard_map.81 = (bf16[4,24,512]{2,1,0:T(8,128)(2,1)}, bf16[4,24,512]{2,1,0:T(8,128)(2,1)}) custom-call(bf16[2,8,2,768]{3,2,1,0:T(2,128)(2,1)S(1)} %collective-permute-done.4.yf, bf16[2,8,2,768]{3,2,1,0:T(2,128)(2,1)S(1)} %collective-permute-done.5.yn, f32[1,320,256]{2,1,0:T(8,128)S(1)} %get-tuple-element.14.mid, f32[2,320,256]{2,1,0:T(8,128)S(1)} %shard_map.80.ends, ...), custom_call_target="tpu_custom_call" | custom-call | tf_op jit(solution)/shard_map/pallas_call | solution.py:306
  (6 shorter events, 0.1 us)
Async XLA Ops:
  1.5 12.6 %collective-permute-start = (bf16[2,4,24,128]{3,2,1,0:T(8,128)(2,1)S(1)}, bf16[2,4,24,128]{3,2,1,0:T(8,128)(2,1)S(1)}, u32[]{:S(2)}, u32[]{:S(2)}) collective-permute-start(bf16[2,4,24,128]{3,2,1,0:T(8,128)(2,1)S(1)} %get-tuple-element.10), channel_id=1, source_target_pairs={{1,2},{3,4},{5,6},{7,8},{9,10},{11,12},{13,14},{2,1},{4,3},{6,5},{... | collective-permute-start | bytes 147464 | tf_op jit(solution)/shard_map/ppermute | solution.py:33
  10.5 6.0 %collective-permute-start.1 = (bf16[2,4,24,128]{3,2,1,0:T(8,128)(2,1)S(1)}, bf16[2,4,24,128]{3,2,1,0:T(8,128)(2,1)S(1)}, u32[]{:S(2)}, u32[]{:S(2)}) collective-permute-start(bf16[2,4,24,128]{3,2,1,0:T(8,128)(2,1)S(1)} %get-tuple-element.11), channel_id=1, source_target_pairs={{0,1},{2,3},{4,5},{6,7},{8,9},{10,11},{12,13},{14,15},{1,0},{3,2},... | collective-permute-start | bytes 147464 | tf_op jit(solution)/shard_map/ppermute | solution.py:33
  16.6 5.5 %collective-permute-start.2 = (bf16[2,2,24,768]{3,2,1,0:T(8,128)(2,1)S(1)}, bf16[2,2,24,768]{3,2,1,0:T(8,128)(2,1)S(1)}, u32[]{:S(2)}, u32[]{:S(2)}) collective-permute-start(bf16[2,2,24,768]{3,2,1,0:T(8,128)(2,1)S(1)} %get-tuple-element.23), channel_id=1, source_target_pairs={{64,128},{192,256},{320,384},{128,64},{256,192},{384,320},{65,129}... | collective-permute-start | bytes 442376 | tf_op jit(solution)/shard_map/ppermute | solution.py:33
  17.3 5.8 %collective-permute-start.3 = (bf16[2,2,24,768]{3,2,1,0:T(8,128)(2,1)S(1)}, bf16[2,2,24,768]{3,2,1,0:T(8,128)(2,1)S(1)}, u32[]{:S(2)}, u32[]{:S(2)}) collective-permute-start(bf16[2,2,24,768]{3,2,1,0:T(8,128)(2,1)S(1)} %get-tuple-element.24), channel_id=1, source_target_pairs={{0,64},{128,192},{256,320},{384,448},{64,0},{192,128},{320,256},{4... | collective-permute-start | bytes 442376 | tf_op jit(solution)/shard_map/ppermute | solution.py:33
  23.3 7.7 %collective-permute-start.4 = (bf16[2,8,2,768]{3,2,1,0:T(2,128)(2,1)S(1)}, bf16[2,8,2,768]{3,2,1,0:T(2,128)(2,1)S(1)}, u32[]{:S(2)}, u32[]{:S(2)}) collective-permute-start(bf16[2,8,2,768]{3,2,1,0:T(2,128)(2,1)S(1)} %bitcast.11), channel_id=1, source_target_pairs={{16,32},{32,16},{17,33},{33,17},{18,34},{34,18},{19,35},{35,19},{2... | collective-permute-start | bytes 147464 | tf_op jit(solution)/shard_map/ppermute | solution.py:33
  27.1 6.0 %collective-permute-start.5 = (bf16[2,8,2,768]{3,2,1,0:T(2,128)(2,1)S(1)}, bf16[2,8,2,768]{3,2,1,0:T(2,128)(2,1)S(1)}, u32[]{:S(2)}, u32[]{:S(2)}) collective-permute-start(bf16[2,8,2,768]{3,2,1,0:T(2,128)(2,1)S(1)} %get-tuple-element.18), channel_id=1, source_target_pairs={{0,16},{32,48},{16,0},{48,32},{1,17},{33,49},{17,1},{49,33},{2,18}... | collective-permute-start | bytes 147464 | tf_op jit(solution)/shard_map/ppermute | solution.py:33

commit v6 on v5

--- a/solution.py
+++ b/solution.py
@@ -173,7 +173,40 @@
     ends[1] = low[(last - 1) * size :]
 
 
-def side_kernel(xl, xr, wa, ends, out, ext, shifted):
+def silu_pair(pre, direction):
+    sig = jax.nn.sigmoid(pre)
+    return pre * sig, sig * (1.0 + pre * (1.0 - sig)) * direction
+
+
+def limit(axis, low, high):
+    at = lax.axis_index(axis)
+    return (
+        jnp.where(at == 0, low, -1),
+        jnp.where(at == lax.axis_size(axis) - 1, high, -1),
+    )
+
+
+def outside_grid(rows, base, planes, pairs):
+    x_low, x_high = limit("gx", 0, planes - 1)
+    z_low, z_high = limit("gz", 0, 1)
+    halves = lax.broadcasted_iota(jnp.int32, rows.shape, 1) // 64
+    first = base | (halves == z_low)
+    final = base | (halves == z_high)
+
+    def at(i, p):
+        drop = first if p == 0 else final if p == pairs - 1 else base
+        if i == 0:
+            drop = drop | (rows * 0 == x_low)
+        if i == planes - 1:
+            drop = drop | (rows * 0 + planes - 1 == x_high)
+        return drop
+
+    return at
+
+
+def main_kernel(
+    xl, xr, wa, wb, bias, mid, ends, partial, total, ext, shifted, hid, again
+):
     ny = xl.shape[2]
     ext[:, :, 0:2, :] = jnp.zeros_like(ext[:, :, 0:2, :])
     ext[:, :, 2 + ny :, :] = jnp.zeros_like(ext[:, :, 2 + ny :, :])
@@ -182,25 +215,58 @@
     shift_rows(ext, shifted)
     read = lambda dy, x, p: shifted[dy, x, :, 128 * p : 128 * p + 256]
     pairs = ext.shape[3] // 128 - 1
-    out[0] = ends[0] + dot(taps(read, [(0, 1)], pairs), columns(wa, (0, 1)))
-    out[1] = ends[1] + dot(taps(read, [(2, 3)], pairs), columns(wa, (2, 3)))
-
-
-def silu_pair(pre, direction):
-    sig = jax.nn.sigmoid(pre)
-    return pre * sig, sig * (1.0 + pre * (1.0 - sig)) * direction
-
-
-def edge_rows(yl, yr, wa, edge, planes, pairs):
-    for f in range(2):
-        edge[:, 4 * f : 4 * f + 2, :] = yl[f]
-        edge[:, 4 * f + 2 : 4 * f + 4, :] = yr[f]
+    planes = hid.shape[1]
+    left = ends[0] + dot(taps(read, [(0, 1)], pairs), columns(wa, (0, 1)))
+    right = ends[1] + dot(taps(read, [(2, 3)], pairs), columns(wa, (2, 3)))
+
+    rows = lax.broadcasted_iota(jnp.int32, (ROWS, 128), 0)
+    drop = outside_grid(rows, (rows < 2) | (rows >= ny), planes, pairs)
+    b = bias[0:1, 0:128]
+    for i in range(planes):
+        k = 128 * (i % 2)
+        for p in range(pairs):
+            fields = []
+            for f in range(2):
+                at = slice((2 * p + f) * ROWS, (2 * p + f + 1) * ROWS)
+                if i < 2:
+                    value = left[at, k : k + 128]
+                elif i >= planes - 2:
+                    value = right[at, k : k + 128]
+                else:
+                    value = mid[i // 2 - 1, at, k : k + 128]
+                lane = slice(128 * p, 128 * p + 128)
+                partial[i, 4 * f : 4 * f + 2, lane] = value[0:2]
+                partial[i, 4 * f + 2 : 4 * f + 4, lane] = value[ny : ny + 2]
+                fields.append(value)
+            for f, value in enumerate(silu_pair(fields[0] + b, fields[1])):
+                hid[f, i, 0:ROWS, 128 * p : 128 * p + 128] = jnp.where(
+                    drop(i, p), 0.0, value
+                )
+
+    for dy in range(3):
+        for x in range(planes):
+            both = jnp.concatenate([hid[f, x, dy : dy + ny, :] for f in range(2)], axis=0)
+            again[dy, x] = both.astype(BF16)
+    read = lambda dy, x, p: again[dy, x, :, 128 * p : 128 * p + 256]
+    blocks = total.shape[0]
+    size = total.shape[1]
+    low = taps(read, [(2 * i, 2 * i + 1) for i in range(blocks)], pairs - 1)
+    high = taps(read, [(2 * i + 2, 2 * i + 3) for i in range(blocks)], pairs - 1)
+    result = dot(low, columns(wb, (0, 1))) + dot(high, columns(wb, (2, 3)))
+    for i in range(blocks):
+        total[i] = result[i * size : i * size + size]
+
+
+def edge_rows(edge, weights, planes, pairs):
     every = edge[...].reshape(edge.shape[0] * 8, edge.shape[2]).astype(BF16)
     lhs = jnp.concatenate(
         [every[:, 128 * p : 128 * p + 256] for p in range(pairs)], axis=0
     )
-    taps_of = lambda dy: [wa[256 * (3 * dx + dy) : 256 * (3 * dx + dy) + 256, :] for dx in range(3)]
-    order = taps_of(0) + taps_of(1) + taps_of(2)
+    order = [
+        weights[256 * (3 * dx + dy) : 256 * (3 * dx + dy) + 256, :]
+        for dy in range(3)
+        for dx in range(3)
+    ]
     parts = [
         dot(lhs, jnp.concatenate(order[:4], axis=1)),
         dot(lhs, jnp.concatenate(order[4:], axis=1)),
@@ -225,81 +291,51 @@
     return out
 
 
-def last_kernel(yf, yn, mid, ends, wa, wb, bias, out, out_t, edge, hid, shifted):
+def last_kernel(yf, yn, partial, total, wa, wb, bias, out, out_t, edge, edge_hid):
     nx, ny, nz = out.shape
     pairs = nz // 128
     yl, yr = pick(is_even("gy"), yf, yn)
-    extra = edge_rows(yl, yr, wa, edge, nx + 2, pairs + 1)
-
-    def limit(axis, low, high):
-        at = lax.axis_index(axis)
-        return (
-            jnp.where(at == 0, low, -1),
-            jnp.where(at == lax.axis_size(axis) - 1, high, -1),
-        )
-
-    x_low, x_high = limit("gx", 0, nx + 1)
-    y_low, y_high = limit("gy", 0, ny + 1)
-    z_low, z_high = limit("gz", 0, 1)
-    rows = lax.broadcasted_iota(jnp.int32, (ROWS, 128), 0)
-    halves = lax.broadcasted_iota(jnp.int32, (ROWS, 128), 1) // 64
-    by_row = (rows == y_low) | (rows == y_high)
-    first = by_row | (halves == z_low)
-    final = by_row | (halves == z_high)
-    first_row = lax.broadcasted_iota(jnp.int32, (8, 128), 0) < 2
+    for f in range(2):
+        edge[:, 4 * f : 4 * f + 2, :] = yl[f]
+        edge[:, 4 * f + 2 : 4 * f + 4, :] = yr[f]
+    extra = edge_rows(edge, wa, nx + 2, pairs + 1)
+    row = lax.broadcasted_iota(jnp.int32, (8, 128), 0)
+    y_low, y_high = limit("gy", 0, 3)
+    drop = outside_grid(
+        row, (row % 4 == y_low) | (row % 4 == y_high), nx + 2, pairs + 1
+    )
     b = bias[0:1, 0:128]
     for i in range(nx + 2):
+        for p in range(pairs + 1):
+            lane = slice(128 * p, 128 * p + 128)
+            both = extra[i, p] + partial[i, :, lane]
+            h, ht = silu_pair(both + b, pltpu.roll(both, 4, 0))
+            value = jnp.where(row < 4, h, pltpu.roll(ht, 4, 0))
+            edge_hid[i, :, lane] = jnp.where(drop(i, p), 0.0, value)
+    extra = edge_rows(edge_hid, wb, nx, pairs)
+    b = bias[1:2, 0:128]
+    for i in range(nx):
         k = 128 * (i % 2)
-        if i < 2:
-            source = ends.at[0]
-        elif i >= nx:
-            source = ends.at[1]
-        else:
-            source = mid.at[i // 2 - 1]
-        for p in range(pairs + 1):
+        for p in range(pairs):
+            near = extra[i, p]
+            far = pltpu.roll(near, 4, 0)
             fields = []
             for f in range(2):
-                at = (2 * p + f) * ROWS
-                e = extra[i, p]
-                up = pltpu.roll(e, 4, 0) if f else e
+                at = (2 * p + f) * ny
+                value = total[i // 2, at : at + ny, k : k + 128]
+                top, bottom = (near, far) if f == 0 else (far, near)
                 fields.append(
                     jnp.concatenate(
                         [
-                            source[at : at + 8, k : k + 128] + jnp.where(first_row, up, 0.0),
-                            source[at + 8 : at + ny, k : k + 128],
-                            source[at + ny : at + ROWS, k : k + 128]
-                            + jnp.where(first_row, pltpu.roll(e, 2 if f else 6, 0), 0.0),
+                            value[0:8] + jnp.where(row < 2, top, 0.0),
+                            value[8 : ny - 8],
+                            value[ny - 8 :] + jnp.where(row >= 6, bottom, 0.0),
                         ],
                         axis=0,
                     )
                 )
-            outside = first if p == 0 else final if p == pairs else by_row
-            if i == 0:
-                outside = outside | (rows * 0 == x_low)
-            if i == nx + 1:
-                outside = outside | (rows * 0 + nx + 1 == x_high)
-            for f, value in enumerate(silu_pair(fields[0] + b, fields[1])):
-                hid[f, i, 0:ROWS, 128 * p : 128 * p + 128] = jnp.where(outside, 0.0, value)
-
-    for dy in range(3):
-        for x in range(nx + 2):
-            both = jnp.concatenate([hid[f, x, dy : dy + ny, :] for f in range(2)], axis=0)
-            shifted[dy, x] = both.astype(BF16)
-    read = lambda dy, x, p: shifted[dy, x, :, 128 * p : 128 * p + 256]
-    blocks = nx // 2
-    low = taps(read, [(2 * i, 2 * i + 1) for i in range(blocks)], pairs)
-    high = taps(read, [(2 * i + 2, 2 * i + 3) for i in range(blocks)], pairs)
-    total = dot(low, columns(wb, (0, 1))) + dot(high, columns(wb, (2, 3)))
-    b = bias[1:2, :]
-    for i in range(blocks):
-        for p in range(pairs):
-            at = (i * pairs + p) * 2 * ny
-            value = silu_pair(total[at : at + ny] + b, total[at + ny : at + 2 * ny])
-            for target, part in zip((out, out_t), value):
-                for k in range(2):
-                    target[2 * i + k, :, 128 * p : 128 * p + 128] = part[
-                        :, 128 * k : 128 * k + 128
-                    ].astype(BF16)
+            for target, value in zip((out, out_t), silu_pair(fields[0] + b, fields[1])):
+                target[i, :, 128 * p : 128 * p + 128] = value.astype(BF16)
 
 
 def call(kernel, ins, outs, scratch, args, mib=24):
@@ -361,7 +397,20 @@
         work(nx),
         (own, zl, zr, wa),
     )
-    (outer,) = call(side_kernel, [VM] * 4, [((2, size, 256), F32)], work(4), (xl, xr, wa, ends_own))
+    partial, total = call(
+        main_kernel,
+        [VM] * 7,
+        [
+            ((nx + 2, 8, nz + 128), F32),
+            ((nx // 2, (nz // 128) * 2 * ny, 256), F32),
+        ],
+        work(4)
+        + [
+            pltpu.VMEM((2, nx + 2, ROWS + 8, nz + 128), F32),
+            pltpu.VMEM((3, nx + 2, 2 * ny, nz + 128), BF16),
+        ],
+        (xl, xr, wa, wb, bias, mid, ends_own),
+    )
     block = ((nx, ny, nz), BF16)
     return tuple(
         call(
@@ -370,10 +419,9 @@
             [block, block],
             [
                 pltpu.VMEM((nx + 4, 8, wide), F32),
-                pltpu.VMEM((2, nx + 2, ROWS + 8, nz + 128), F32),
-                pltpu.VMEM((3, nx + 2, 2 * ny, nz + 128), BF16),
+                pltpu.VMEM((nx + 2, 8, nz + 128), F32),
             ],
-            (yf, yn, mid, outer, wa, wb, bias),
+            (yf, yn, partial, total, wa, wb, bias),
         )
     )
 

time: 35.5 us -> 35.7 us (level)
  the two profiles are of different devices: /device:TPU:38 before, /device:TPU:15 now
where the time goes in v6:
time: 35.7 us; the launch traced here: 35.3 us
  starting transfers between devices  24.9 us (70%)
  Pallas kernels  6.77 us (19%)
  waiting for transfers between devices  2.6 us (7%)
  between operations  0.81 us (2%)
    ppermute x6, starting transfers between devices, send(): return lax.ppermute(operand, axis, both_ways(pairs))  24.9 us
    pallas_call x5, Pallas kernels, call(): pl.pallas_call(kernel, in_specs=ins, out_specs=[VM] * len(outs), out_shap...  6.77 us
    ppermute x6, waiting for transfers between devices, send(): return lax.ppermute(operand, axis, both_ways(pairs))  2.6 us
  transfers between devices with their start and end apart: 6, of which 3 were waited for; matrix products, arithmetic and copies ran while one was open for 0% of the time, Pallas kernels for 13%

profile of v6, /device:TPU:15, one launch (start us, length us, event | category | flops | bytes accessed | tf_op | source)
XLA Modules:
  0.0 35.3 jit_solution(6781762539964820944)
XLA Ops:
  0.6 0.9 %shard_map.77 = (bf16[2,4,24,128]{3,2,1,0:T(8,128)(2,1)S(1)}, bf16[2,4,24,128]{3,2,1,0:T(8,128)(2,1)S(1)}) custom-call(bf16[4,24,512]{2,1,0:T(8,128)(2,1)} %src.3, bf16[4,24,512]{2,1,0:T(8,128)(2,1)} %tan.3), custom_call_target="tpu_custom_call" | custom-call | tf_op jit(solution)/shard_map/pallas_call | solution.py:342
  1.5 8.7 %collective-permute-start = (bf16[2,4,24,128]{3,2,1,0:T(8,128)(2,1)S(1)}, bf16[2,4,24,128]{3,2,1,0:T(8,128)(2,1)S(1)}, u32[]{:S(2)}, u32[]{:S(2)}) collective-permute-start(bf16[2,4,24,128]{3,2,1,0:T(8,128)(2,1)S(1)} %get-tuple-element.12), channel_id=1, source_target_pairs={{1,2},{3,4},{5,6},{7,8},{9,10},{11,12},{13,14},{2,1},{4,3},{6,5},{... | collective-permute-start | bytes 147464 | tf_op jit(solution)/shard_map/ppermute | solution.py:33
  10.2 1.9 %collective-permute-start.1 = (bf16[2,4,24,128]{3,2,1,0:T(8,128)(2,1)S(1)}, bf16[2,4,24,128]{3,2,1,0:T(8,128)(2,1)S(1)}, u32[]{:S(2)}, u32[]{:S(2)}) collective-permute-start(bf16[2,4,24,128]{3,2,1,0:T(8,128)(2,1)S(1)} %get-tuple-element.13), channel_id=1, source_target_pairs={{0,1},{2,3},{4,5},{6,7},{8,9},{10,11},{12,13},{14,15},{1,0},{3,2},... | collective-permute-start | bytes 147464 | tf_op jit(solution)/shard_map/ppermute | solution.py:33
  12.2 1.6 %shard_map.78 = (bf16[2,4,24,512]{3,2,1,0:T(8,128)(2,1)S(1)}, bf16[2304,128]{1,0:T(8,128)(2,1)S(1)}, bf16[2304,128]{1,0:T(8,128)(2,1)S(1)}, f32[2,256]{1,0:T(2,128)S(1)}) custom-call(bf16[4,24,512]{2,1,0:T(8,128)(2,1)} %src.3, bf16[4,24,512]{2,1,0:T(8,128)(2,1)} %tan.3, bf16[9,192,64]{2,1,0:T(8,128)(2,1)} %bitcast.7, bf16[9,192,64]{2,1,0:T(8,128)(2,1)} %bitcast.8, ...), custom_call_target="tpu_custom_call" | custom-call | tf_op jit(solution)/shard_map/pallas_call | solution.py:342
  13.8 0.0 collective-permute-done
  13.8 1.3 %collective-permute-done.1 = bf16[2,4,24,128]{3,2,1,0:T(8,128)(2,1)S(1)} collective-permute-done((bf16[2,4,24,128]{3,2,1,0:T(8,128)(2,1)S(1)}, bf16[2,4,24,128]{3,2,1,0:T(8,128)(2,1)S(1)}, u32[]{:S(2)}, u32[]{:S(2)}) %collective-permute-start.1) | collective-permute-done | bytes 49184 | tf_op jit(solution)/shard_map/ppermute | solution.py:33
  15.2 5.2 %collective-permute-start.2 = (bf16[2,2,24,768]{3,2,1,0:T(8,128)(2,1)S(1)}, bf16[2,2,24,768]{3,2,1,0:T(8,128)(2,1)S(1)}, u32[]{:S(2)}, u32[]{:S(2)}) collective-permute-start(bf16[2,2,24,768]{3,2,1,0:T(8,128)(2,1)S(1)} %get-tuple-element.27), channel_id=1, source_target_pairs={{64,128},{192,256},{320,384},{128,64},{256,192},{384,320},{65,129}... | collective-permute-start | bytes 442376 | tf_op jit(solution)/shard_map/ppermute | solution.py:33
  20.4 1.9 %collective-permute-start.3 = (bf16[2,2,24,768]{3,2,1,0:T(8,128)(2,1)S(1)}, bf16[2,2,24,768]{3,2,1,0:T(8,128)(2,1)S(1)}, u32[]{:S(2)}, u32[]{:S(2)}) collective-permute-start(bf16[2,2,24,768]{3,2,1,0:T(8,128)(2,1)S(1)} %get-tuple-element.28), channel_id=1, source_target_pairs={{0,64},{128,192},{256,320},{384,448},{64,0},{192,128},{320,256},{4... | collective-permute-start | bytes 442376 | tf_op jit(solution)/shard_map/ppermute | solution.py:33
  22.3 1.0 %collective-permute-done.2 = bf16[2,2,24,768]{3,2,1,0:T(8,128)(2,1)S(1)} collective-permute-done((bf16[2,2,24,768]{3,2,1,0:T(8,128)(2,1)S(1)}, bf16[2,2,24,768]{3,2,1,0:T(8,128)(2,1)S(1)}, u32[]{:S(2)}, u32[]{:S(2)}) %collective-permute-start.2) | collective-permute-done | bytes 147488 | tf_op jit(solution)/shard_map/ppermute | solution.py:33
  23.3 0.3 collective-permute-done.3
  23.7 0.1 broadcast_select_fusion.4
  23.8 0.7 %collective-permute-start.4 = (bf16[2,8,2,768]{3,2,1,0:T(2,128)(2,1)S(1)}, bf16[2,8,2,768]{3,2,1,0:T(2,128)(2,1)S(1)}, u32[]{:S(2)}, u32[]{:S(2)}) collective-permute-start(bf16[2,8,2,768]{3,2,1,0:T(2,128)(2,1)S(1)} %bitcast.11), channel_id=1, source_target_pairs={{16,32},{32,16},{17,33},{33,17},{18,34},{34,18},{19,35},{35,19},{2... | collective-permute-start | bytes 147464 | tf_op jit(solution)/shard_map/ppermute | solution.py:33
  24.5 6.4 %collective-permute-start.5 = (bf16[2,8,2,768]{3,2,1,0:T(2,128)(2,1)S(1)}, bf16[2,8,2,768]{3,2,1,0:T(2,128)(2,1)S(1)}, u32[]{:S(2)}, u32[]{:S(2)}) collective-permute-start(bf16[2,8,2,768]{3,2,1,0:T(2,128)(2,1)S(1)} %get-tuple-element.22), channel_id=1, source_target_pairs={{0,16},{32,48},{16,0},{48,32},{1,17},{33,49},{17,1},{49,33},{2,18}... | collective-permute-start | bytes 147464 | tf_op jit(solution)/shard_map/ppermute | solution.py:33
  30.9 1.2 %shard_map.79 = (f32[1,320,256]{2,1,0:T(8,128)S(1)}, f32[2,320,256]{2,1,0:T(8,128)S(1)}) custom-call(bf16[2,4,24,512]{3,2,1,0:T(8,128)(2,1)S(1)} %get-tuple-element.14.own, bf16[2,4,24,128]{3,2,1,0:T(8,128)(2,1)S(1)} %get-tuple-element.33.zl, bf16[2,4,24,128]{3,2,1,0:T(8,128)(2,1)S(1)} %get-tuple-element.34.zr, bf16[2304,128]{1,0:T(8,128)(2,1)S(1)} %get-tuple-element.15.wa), custom_call_target="tpu_custom_call" | custom-call | tf_op jit(solution)/shard_map/pallas_call | solution.py:342
  32.2 1.6 %shard_map.80 = (f32[6,8,640]{2,1,0:T(8,128)S(1)}, f32[2,192,256]{2,1,0:T(8,128)S(1)}) custom-call(bf16[2,2,24,768]{3,2,1,0:T(8,128)(2,1)S(1)} %get-tuple-element.25.xl, bf16[2,2,24,768]{3,2,1,0:T(8,128)(2,1)S(1)} %get-tuple-element.26.xr, bf16[2304,128]{1,0:T(8,128)(2,1)S(1)} %get-tuple-element.15.wa, bf16[2304,128]{1,0:T(8,128)(2,1)S(1)} %get-tuple-element.16.wb, ...), custom_call_target="tpu_custom_call" | custom-call | tf_op jit(solution)/shard_map/pallas_call | solution.py:342
  33.8 0.0 collective-permute-done.4.yf
  33.8 0.0 collective-permute-done.5.yn
  33.9 1.4 %shard_map.81 = (bf16[4,24,512]{2,1,0:T(8,128)(2,1)}, bf16[4,24,512]{2,1,0:T(8,128)(2,1)}) custom-call(bf16[2,8,2,768]{3,2,1,0:T(2,128)(2,1)S(1)} %collective-permute-done.4.yf, bf16[2,8,2,768]{3,2,1,0:T(2,128)(2,1)S(1)} %collective-permute-done.5.yn, f32[6,8,640]{2,1,0:T(8,128)S(1)} %get-tuple-element.20.partial, ...), custom_call_target="tpu_custom_call" | custom-call | tf_op jit(solution)/shard_map/pallas_call | solution.py:342
  (6 shorter events, 0.1 us)
Async XLA Ops:
  1.5 12.3 %collective-permute-start = (bf16[2,4,24,128]{3,2,1,0:T(8,128)(2,1)S(1)}, bf16[2,4,24,128]{3,2,1,0:T(8,128)(2,1)S(1)}, u32[]{:S(2)}, u32[]{:S(2)}) collective-permute-start(bf16[2,4,24,128]{3,2,1,0:T(8,128)(2,1)S(1)} %get-tuple-element.12), channel_id=1, source_target_pairs={{1,2},{3,4},{5,6},{7,8},{9,10},{11,12},{13,14},{2,1},{4,3},{6,5},{... | collective-permute-start | bytes 147464 | tf_op jit(solution)/shard_map/ppermute | solution.py:33
  10.2 4.8 %collective-permute-start.1 = (bf16[2,4,24,128]{3,2,1,0:T(8,128)(2,1)S(1)}, bf16[2,4,24,128]{3,2,1,0:T(8,128)(2,1)S(1)}, u32[]{:S(2)}, u32[]{:S(2)}) collective-permute-start(bf16[2,4,24,128]{3,2,1,0:T(8,128)(2,1)S(1)} %get-tuple-element.13), channel_id=1, source_target_pairs={{0,1},{2,3},{4,5},{6,7},{8,9},{10,11},{12,13},{14,15},{1,0},{3,2},... | collective-permute-start | bytes 147464 | tf_op jit(solution)/shard_map/ppermute | solution.py:33
  15.2 8.2 %collective-permute-start.2 = (bf16[2,2,24,768]{3,2,1,0:T(8,128)(2,1)S(1)}, bf16[2,2,24,768]{3,2,1,0:T(8,128)(2,1)S(1)}, u32[]{:S(2)}, u32[]{:S(2)}) collective-permute-start(bf16[2,2,24,768]{3,2,1,0:T(8,128)(2,1)S(1)} %get-tuple-element.27), channel_id=1, source_target_pairs={{64,128},{192,256},{320,384},{128,64},{256,192},{384,320},{65,129}... | collective-permute-start | bytes 442376 | tf_op jit(solution)/shard_map/ppermute | solution.py:33
  20.4 3.3 %collective-permute-start.3 = (bf16[2,2,24,768]{3,2,1,0:T(8,128)(2,1)S(1)}, bf16[2,2,24,768]{3,2,1,0:T(8,128)(2,1)S(1)}, u32[]{:S(2)}, u32[]{:S(2)}) collective-permute-start(bf16[2,2,24,768]{3,2,1,0:T(8,128)(2,1)S(1)} %get-tuple-element.28), channel_id=1, source_target_pairs={{0,64},{128,192},{256,320},{384,448},{64,0},{192,128},{320,256},{4... | collective-permute-start | bytes 442376 | tf_op jit(solution)/shard_map/ppermute | solution.py:33
  23.8 10.0 %collective-permute-start.4 = (bf16[2,8,2,768]{3,2,1,0:T(2,128)(2,1)S(1)}, bf16[2,8,2,768]{3,2,1,0:T(2,128)(2,1)S(1)}, u32[]{:S(2)}, u32[]{:S(2)}) collective-permute-start(bf16[2,8,2,768]{3,2,1,0:T(2,128)(2,1)S(1)} %bitcast.11), channel_id=1, source_target_pairs={{16,32},{32,16},{17,33},{33,17},{18,34},{34,18},{19,35},{35,19},{2... | collective-permute-start | bytes 147464 | tf_op jit(solution)/shard_map/ppermute | solution.py:33
  24.5 9.3 %collective-permute-start.5 = (bf16[2,8,2,768]{3,2,1,0:T(2,128)(2,1)S(1)}, bf16[2,8,2,768]{3,2,1,0:T(2,128)(2,1)S(1)}, u32[]{:S(2)}, u32[]{:S(2)}) collective-permute-start(bf16[2,8,2,768]{3,2,1,0:T(2,128)(2,1)S(1)} %get-tuple-element.22), channel_id=1, source_target_pairs={{0,16},{32,48},{16,0},{48,32},{1,17},{33,49},{17,1},{49,33},{2,18}... | collective-permute-start | bytes 147464 | tf_op jit(solution)/shard_map/ppermute | solution.py:33
